TPU v7x, 32 devices: a whole 2x2x4 slice. The times are simulated.
32 devices in a mesh: dp: 16 (over z, y, core), tensor: 2 (over x).
Axes of the slice: x: 2, y: 2, z: 4, core: 2. Of those that a mesh axis runs over, the one named last changes fastest.
Arguments:
- tokens: bfloat16 [16384, 1024], P('dp'), may hold values from -6 to 6
- segment_ids: int32 [16, 1024], P('dp'), may hold values from 0 to 4, never falling along the last dimension, each value on 1 to 384 neighbouring positions
- decay_rate: float32 [8], P('tensor'), may hold values from 0.00029296876 to 0.08
- query_weight: bfloat16 [1024, 1024], P(None, 'tensor'), may hold values from -0.1875 to 0.1875
- key_weight: bfloat16 [1024, 1024], P(None, 'tensor'), may hold values from -0.1875 to 0.1875
- value_weight: bfloat16 [1024, 1024], P(None, 'tensor'), may hold values from -0.1875 to 0.1875
- gate_weight: bfloat16 [1024, 1024], P(None, 'tensor'), may hold values from -0.1875 to 0.1875
- output_weight: bfloat16 [1024, 1024], P('tensor'), may hold values from -0.1875 to 0.1875
- norm_gain: bfloat16 [8, 128], P('tensor'), may hold values from 0.099609375 to 1.8984375
- left_weight: bfloat16 [1024, 2816], P(None, 'tensor'), may hold values from -0.1875 to 0.1875
- right_weight: bfloat16 [1024, 2816], P(None, 'tensor'), may hold values from -0.1875 to 0.1875
- down_weight: bfloat16 [2816, 1024], P('tensor'), may hold values from -0.109375 to 0.109375
- cotangent: bfloat16 [16384, 1024], P('dp'), may hold values from -6 to 6
Outputs:
- block_out: bfloat16 [16384, 1024], P('dp')
- tokens_grad: float32 [16384, 1024], P('dp')
- query_grad: float32 [1024, 1024], P('dp', 'tensor')
- key_grad: float32 [1024, 1024], P('dp', 'tensor')
- value_grad: float32 [1024, 1024], P('dp', 'tensor')
- gate_grad: float32 [1024, 1024], P('dp', 'tensor')
- output_grad: float32 [1024, 1024], P('tensor', 'dp')
- gain_grad: float32 [8, 128], P('tensor', 'dp')
- left_grad: float32 [1024, 2816], P('dp', 'tensor')
- right_grad: float32 [1024, 2816], P('dp', 'tensor')
- down_grad: float32 [2816, 1024], P('tensor', 'dp')
Inputs may be any that keep to these rules, and one draw needn't show every extreme that they name: `segment_ids`: along each packed sequence the ids never fall; a document holds at most 384 tokens, and some document holds exactly that many.
All inputs are finite; a program needn't handle non-finite values.
Results may differ from a plain program's by a relative error of at most 0.014.
Values may be sent and summed in bfloat16 or wider, within the bound.
A program may use at most 192 MiB of HBM per device.

v0:
```python
import jax
import jax.numpy as jnp
from jax import lax
from jax.sharding import PartitionSpec as P

eps = 1e-06


def product(left_op, right_op):
    return jnp.dot(left_op, right_op, preferred_element_type=jnp.float32)


def product_tn(left_op, right_op):
    return lax.dot_general(
        left_op, right_op, (((0,), (0,)), ((), ())), preferred_element_type=jnp.float32
    )


def product_nt(left_op, right_op):
    return lax.dot_general(
        left_op, right_op, (((1,), (1,)), ((), ())), preferred_element_type=jnp.float32
    )


def rms_scale(values):
    return lax.rsqrt(jnp.mean(values * values, axis=1, keepdims=True) + eps)


def rms_back(values, scale, grads):
    return scale * grads - values * (scale * scale * scale) * jnp.mean(
        values * grads, axis=1, keepdims=True
    )


def silu_slope(values):
    sigma = jax.nn.sigmoid(values)
    return sigma * (1.0 + values * (1.0 - sigma))


def tensor_sum(values):
    return lax.psum(values, "tensor")


def row_stat(values):
    return lax.psum(values, "tensor")


def decay_mask(segment, decays, offset, height):
    length = segment.shape[0]
    rows_at = offset + jnp.arange(height)
    cols_at = jnp.arange(length)
    distance = rows_at[:, None] - cols_at[None, :]
    same_doc = segment[offset : offset + height][:, None] == segment[None, :]
    allowed = (distance >= 0) & same_doc
    falloff = jnp.exp(-decays[:, None, None] * jnp.maximum(distance, 0).astype(jnp.float32)[None])
    return jnp.where(allowed[None], falloff, jnp.float32(0.0))


def forward_heads(queries, key_rows, value_rows, segments, decays):
    length = segments.shape[1]
    height = min(512, length)

    def forward_one_sequence(entries):
        seq_query, seq_key, seq_value, segment = entries
        outputs = []
        for offset in range(0, length, height):
            masking = decay_mask(segment, decays, offset, height)
            scores = jnp.einsum(
                "qhd,khd->hqk",
                seq_query[offset : offset + height],
                seq_key,
                preferred_element_type=jnp.float32,
            )
            weighted = (scores * masking).astype(jnp.bfloat16)
            outputs.append(
                jnp.einsum("hqk,khd->qhd", weighted, seq_value, preferred_element_type=jnp.float32)
            )
        return jnp.concatenate(outputs, axis=0)

    return lax.map(forward_one_sequence, (queries, key_rows, value_rows, segments))


def backward_heads(queries, key_rows, value_rows, segments, grad_heads, decays):
    length = segments.shape[1]
    height = min(512, length)

    def backward_one_sequence(entries):
        seq_query, seq_key, seq_value, segment, seq_grad = entries
        grad_key = jnp.zeros(seq_key.shape, jnp.float32)
        grad_value = jnp.zeros(seq_value.shape, jnp.float32)
        grad_parts = []
        for offset in range(0, length, height):
            masking = decay_mask(segment, decays, offset, height)
            rows_query = seq_query[offset : offset + height]
            rows_grad = seq_grad[offset : offset + height]
            scores = jnp.einsum(
                "qhd,khd->hqk", rows_query, seq_key, preferred_element_type=jnp.float32
            )
            weighted = (scores * masking).astype(jnp.bfloat16)
            grad_weighted = jnp.einsum(
                "qhd,khd->hqk", rows_grad, seq_value, preferred_element_type=jnp.float32
            )
            grad_scores = (grad_weighted * masking).astype(jnp.bfloat16)
            grad_parts.append(
                jnp.einsum("hqk,khd->qhd", grad_scores, seq_key, preferred_element_type=jnp.float32)
            )
            grad_key = grad_key + jnp.einsum(
                "hqk,qhd->khd", grad_scores, rows_query, preferred_element_type=jnp.float32
            )
            grad_value = grad_value + jnp.einsum(
                "hqk,qhd->khd", weighted, rows_grad, preferred_element_type=jnp.float32
            )
        return (jnp.concatenate(grad_parts, axis=0), grad_key, grad_value)

    return lax.map(backward_one_sequence, (queries, key_rows, value_rows, segments, grad_heads))


def local(
    tokens,
    segment_ids,
    decay_rate,
    query_weight,
    key_weight,
    value_weight,
    gate_weight,
    output_weight,
    norm_gain,
    left_weight,
    right_weight,
    down_weight,
    cotangent,
):
    seq_count, length = segment_ids.shape
    local_heads, head_size = norm_gain.shape
    rows_total = tokens.shape[0]
    inner_width = local_heads * head_size
    full_inner = inner_width * lax.axis_size("tensor")
    gain_flat = norm_gain.astype(jnp.float32).reshape(inner_width)

    def by_head(values):
        return values.reshape(seq_count, length, local_heads, head_size)

    source = tokens.astype(jnp.float32)
    scale_in = rms_scale(source)
    normed = (source * scale_in).astype(jnp.bfloat16)
    pre_query = product(normed, query_weight)
    pre_key = product(normed, key_weight)
    queries = jax.nn.silu(pre_query).astype(jnp.bfloat16)
    key_rows = jax.nn.silu(pre_key).astype(jnp.bfloat16)
    value_rows = product(normed, value_weight).astype(jnp.bfloat16)
    gate_act = product(normed, gate_weight)
    heads_out = forward_heads(
        by_head(queries), by_head(key_rows), by_head(value_rows), segment_ids, decay_rate
    ).reshape(rows_total, inner_width)
    square_total = row_stat(jnp.sum(heads_out * heads_out, axis=1))
    scale_out = lax.rsqrt(square_total / full_inner + eps)[:, None]
    normed_heads = heads_out * scale_out
    scaled_heads = normed_heads * gain_flat
    mixed = (scaled_heads * gate_act).astype(jnp.bfloat16)
    attn_part = product(mixed, output_weight)
    hidden = source + tensor_sum(attn_part)
    scale_mid = rms_scale(hidden)
    lifted = (hidden * scale_mid).astype(jnp.bfloat16)
    left_act = product(lifted, left_weight)
    right_act = product(lifted, right_weight)
    joined = (left_act * right_act).astype(jnp.bfloat16)
    down_part = product(joined, down_weight)
    block_out = (hidden + tensor_sum(down_part)).astype(jnp.bfloat16)
    grad_joined = product_nt(cotangent, down_weight)
    down_grad = product_tn(joined, cotangent)
    grad_left = (grad_joined * right_act).astype(jnp.bfloat16)
    grad_right = (grad_joined * left_act).astype(jnp.bfloat16)
    left_grad = product_tn(lifted, grad_left)
    right_grad = product_tn(lifted, grad_right)
    lifted_part = product_nt(grad_left, left_weight) + product_nt(grad_right, right_weight)
    grad_hidden = cotangent.astype(jnp.float32) + rms_back(
        hidden, scale_mid, tensor_sum(lifted_part)
    )
    grad_low = grad_hidden.astype(jnp.bfloat16)
    output_grad = product_tn(mixed, grad_low)
    grad_mixed = product_nt(grad_low, output_weight)
    grad_scaled = grad_mixed * gate_act
    grad_gate = (grad_mixed * scaled_heads).astype(jnp.bfloat16)
    gain_grad = jnp.sum(grad_scaled * normed_heads, axis=0).reshape(local_heads, head_size)
    grad_normed = grad_scaled * gain_flat
    cross_total = row_stat(jnp.sum(heads_out * grad_normed, axis=1))[:, None]
    grad_heads = (
        scale_out * grad_normed
        - heads_out * (scale_out * scale_out * scale_out) * (cross_total / full_inner)
    ).astype(jnp.bfloat16)
    grad_query, grad_key, grad_value = backward_heads(
        by_head(queries),
        by_head(key_rows),
        by_head(value_rows),
        segment_ids,
        by_head(grad_heads),
        decay_rate,
    )
    query_pull = (grad_query.reshape(rows_total, inner_width) * silu_slope(pre_query)).astype(
        jnp.bfloat16
    )
    key_pull = (grad_key.reshape(rows_total, inner_width) * silu_slope(pre_key)).astype(
        jnp.bfloat16
    )
    value_pull = grad_value.reshape(rows_total, inner_width).astype(jnp.bfloat16)
    query_grad = product_tn(normed, query_pull)
    key_grad = product_tn(normed, key_pull)
    value_grad = product_tn(normed, value_pull)
    gate_grad = product_tn(normed, grad_gate)
    normed_part = (
        product_nt(query_pull, query_weight)
        + product_nt(key_pull, key_weight)
        + product_nt(value_pull, value_weight)
        + product_nt(grad_gate, gate_weight)
    )
    tokens_grad = grad_hidden + rms_back(source, scale_in, tensor_sum(normed_part))
    (
        query_total,
        key_total,
        value_total,
        gate_total,
        left_total,
        right_total,
        output_total,
        down_total,
        gain_total,
    ) = (
        lax.psum_scatter(query_grad, "dp", scatter_dimension=0, tiled=True),
        lax.psum_scatter(key_grad, "dp", scatter_dimension=0, tiled=True),
        lax.psum_scatter(value_grad, "dp", scatter_dimension=0, tiled=True),
        lax.psum_scatter(gate_grad, "dp", scatter_dimension=0, tiled=True),
        lax.psum_scatter(left_grad, "dp", scatter_dimension=0, tiled=True),
        lax.psum_scatter(right_grad, "dp", scatter_dimension=0, tiled=True),
        lax.psum_scatter(output_grad, "dp", scatter_dimension=1, tiled=True),
        lax.psum_scatter(down_grad, "dp", scatter_dimension=1, tiled=True),
        lax.psum_scatter(gain_grad, "dp", scatter_dimension=1, tiled=True),
    )
    return (
        block_out,
        tokens_grad,
        query_total,
        key_total,
        value_total,
        gate_total,
        output_total,
        gain_total,
        left_total,
        right_total,
        down_total,
    )


def solution(mesh):
    in_specs = (
        P("dp", None),
        P("dp", None),
        P("tensor"),
        P(None, "tensor"),
        P(None, "tensor"),
        P(None, "tensor"),
        P(None, "tensor"),
        P("tensor", None),
        P("tensor", None),
        P(None, "tensor"),
        P(None, "tensor"),
        P("tensor", None),
        P("dp", None),
    )
    out_specs = (
        P("dp", None),
        P("dp", None),
        P("dp", "tensor"),
        P("dp", "tensor"),
        P("dp", "tensor"),
        P("dp", "tensor"),
        P("tensor", "dp"),
        P("tensor", "dp"),
        P("dp", "tensor"),
        P("dp", "tensor"),
        P("tensor", "dp"),
    )
    return jax.shard_map(local, mesh=mesh, in_specs=in_specs, out_specs=out_specs, check_vma=False)
```

profile of v0, /device:TPU:0, one launch (start us, length us, event | category | flops | bytes accessed | tf_op | source)
XLA Modules:
  0.0 1135.4 jit_solution(16612577454618419392)
XLA Ops:
  31.9 6.0 psum.42
  38.0 5.4 multiply_convert_fusion.9
  47.7 109.7 %all-reduce.6.cloned.1.call-done = f32[1024,1024]{1,0:T(8,128)} async-done(((f32[1024,1024]{1,0:T(8,128)}), f32[1024,1024]{1,0:T(8,128)}) %all-reduce.6.cloned.1.call-update) | async-done | bytes 4194320 | tf_op jit(solution)/shard_map/psum | solution.py:41
  170.9 6.0 multiply_convert_fusion.4
  176.8 6.3 fusion.43
  183.1 5.0 convolution_add_fusion
  188.6 6.8 fusion.42
  195.4 100.8 %all-reduce.8.cloned.1.call-done = f32[1024,1024]{1,0:T(8,128)} async-done(((f32[1024,1024]{1,0:T(8,128)}), f32[1024,1024]{1,0:T(8,128)}) %all-reduce.8.cloned.1.call-update) | async-done | bytes 4194320 | tf_op jit(solution)/shard_map/psum | solution.py:41
  309.3 4.9 psum.46
  355.6 5.2 fusion.17
  369.2 8.7 fusion.49
  378.0 8.6 fusion.50
  387.0 8.4 fusion.51
  397.2 31.7 %all-reduce = f32[4,128]{1,0:T(4,128)S(1)} all-reduce(f32[4,128]{1,0:T(4,128)S(1)} %bitcast.138), channel_id=7, replica_groups=mesh['dp'=16,'tensor'=2] {'dp'}, use_global_device_ids=true, to_apply=%region_18.19.clone | all-reduce | flops 512 | bytes 4096
  429.6 115.7 %all-reduce.10.cloned.1.call-done = (f32[1024,1024]{1,0:T(8,128)}, f32[1024,1024]{1,0:T(8,128)}) async-done(((f32[1024,1024]{1,0:T(8,128)}, f32[1024,1024]{1,0:T(8,128)}), (f32[1024,1024]{1,0:T(8,128)}, f32[1024,1024]{1,0:T(8,128)})) %all-reduce.10.cloned.1.call-update) | async-done | bytes 8388624 | tf_op jit(solution)/shard_map/psum | solution.py:41
  549.4 7.3 fusion.4
  556.8 54.6 %reduce-scatter.12.cloned.1.call-done = f32[64,512]{1,0:T(8,128)} async-done(((f32[1024,512]{1,0:T(8,128)}), f32[64,512]{1,0:T(8,128)}) %reduce-scatter.12.cloned.1.call-update) | async-done | bytes 131088 | tf_op jit(solution)/shard_map/reduce_scatter | solution.py:229
  611.4 65.2 %reduce-scatter.10.cloned.1.call-done = f32[64,512]{1,0:T(8,128)} async-done(((f32[1024,512]{1,0:T(8,128)}), f32[64,512]{1,0:T(8,128)}) %reduce-scatter.10.cloned.1.call-update) | async-done | bytes 131088 | tf_op jit(solution)/shard_map/reduce_scatter | solution.py:228
  676.7 64.7 %reduce-scatter.18.cloned.1.call-done = f32[512,64]{0,1:T(8,128)} async-done(((f32[512,1024]{0,1:T(8,128)}), f32[512,64]{0,1:T(8,128)}) %reduce-scatter.18.cloned.1.call-update) | async-done | bytes 131088 | tf_op jit(solution)/shard_map/reduce_scatter | solution.py:234
  741.4 65.3 %reduce-scatter.14.cloned.1.call-done = f32[64,512]{1,0:T(8,128)} async-done(((f32[1024,512]{1,0:T(8,128)}), f32[64,512]{1,0:T(8,128)}) %reduce-scatter.14.cloned.1.call-update) | async-done | bytes 131088 | tf_op jit(solution)/shard_map/reduce_scatter | solution.py:230
  806.7 64.9 %reduce-scatter.16.cloned.1.call-done = f32[64,512]{1,0:T(8,128)} async-done(((f32[1024,512]{1,0:T(8,128)}), f32[64,512]{1,0:T(8,128)}) %reduce-scatter.16.cloned.1.call-update) | async-done | bytes 131088 | tf_op jit(solution)/shard_map/reduce_scatter | solution.py:231
  871.6 85.6 %reduce-scatter.20.cloned.1.call-done = f32[64,1408]{1,0:T(8,128)} async-done(((f32[1024,1408]{1,0:T(8,128)}), f32[64,1408]{1,0:T(8,128)}) %reduce-scatter.20.cloned.1.call-update) | async-done | bytes 360464 | tf_op jit(solution)/shard_map/reduce_scatter | solution.py:232
  957.1 85.5 %reduce-scatter.22.cloned.1.call-done = f32[64,1408]{1,0:T(8,128)} async-done(((f32[1024,1408]{1,0:T(8,128)}), f32[64,1408]{1,0:T(8,128)}) %reduce-scatter.22.cloned.1.call-update) | async-done | bytes 360464 | tf_op jit(solution)/shard_map/reduce_scatter | solution.py:233
  1042.7 85.7 %reduce-scatter.24.cloned.1.call-done = f32[1408,64]{0,1:T(8,128)} async-done(((f32[1408,1024]{0,1:T(8,128)}), f32[1408,64]{0,1:T(8,128)}) %reduce-scatter.24.cloned.1.call-update) | async-done | bytes 360464 | tf_op jit(solution)/shard_map/reduce_scatter | solution.py:235
  (193 shorter events, 111.6 us)
Async XLA Ops:
  7.2 163.7 %copy-start = (bf16[1408,1024]{1,0:T(8,128)(2,1)S(1)}, bf16[1408,1024]{1,0:T(8,128)(2,1)}, u32[]{:S(2)}) copy-start(bf16[1408,1024]{1,0:T(8,128)(2,1)} %param.24) | copy-start | bytes 8650756
  7.2 150.3 %all-reduce.6.cloned.1.call-start = ((), (), s32[]{:S(2)}) async-start(), calls=%async_computation.8 | async-start | bytes 8388608 | tf_op jit(solution)/shard_map/psum | solution.py:41
  9.0 16.4 %copy-start.35 = (f32[512,1024]{1,0:T(8,128)}, f32[512,1024]{1,0:T(8,128)S(1)}, u32[]{:S(2)}) copy-start(f32[512,1024]{1,0:T(8,128)S(1)} %maximum_convert_fusion.1) | copy-start | bytes 6291460
  13.3 12.1 %copy-start.23 = (bf16[1024,512]{0,1:T(8,128)(2,1)}, bf16[1024,512]{0,1:T(8,128)(2,1)S(1)}, u32[]{:S(2)}) copy-start(bf16[1024,512]{0,1:T(8,128)(2,1)S(1)} %get-tuple-element.90) | copy-start | bytes 3145732
  16.4 9.0 copy-start.27
  19.1 9.1 copy-start.25
  30.3 7.7 copy-start.46
  38.0 6.4 copy-start.20
  47.7 248.5 %all-reduce.8.cloned.1.call-start = ((), (), s32[]{:S(2)}) async-start(), calls=%async_computation.9 | async-start | bytes 8388608 | tf_op jit(solution)/shard_map/psum | solution.py:41
  176.8 6.3 copy-start.29
  176.8 6.3 copy-start.49
  188.1 357.2 %all-reduce.10.cloned.1.call-start = ((), (), s32[]{:S(2)}) async-start(), calls=%async_computation.18 | async-start | bytes 16777216 | tf_op jit(solution)/shard_map/psum | solution.py:41
  195.4 105.6 %copy-start.4 = (bf16[1024,1024]{1,0:T(8,128)(2,1)S(1)}, bf16[1024,1024]{1,0:T(8,128)(2,1)}, u32[]{:S(2)}) copy-start(bf16[1024,1024]{1,0:T(8,128)(2,1)} %param.13) | copy-start | bytes 6291460
  296.2 5.2 copy-start.7
  296.2 6.5 copy-start.16
  346.6 264.8 %reduce-scatter.12.cloned.1.call-start = ((), (), s32[]{:S(2)}) async-start(), calls=%async_computation.11 | async-start | bytes 2228224 | tf_op jit(solution)/shard_map/reduce_scatter | solution.py:229
  350.9 325.8 %reduce-scatter.10.cloned.1.call-start = ((), (), s32[]{:S(2)}) async-start(), calls=%async_computation.10 | async-start | bytes 2228224 | tf_op jit(solution)/shard_map/reduce_scatter | solution.py:228
  355.6 385.8 %reduce-scatter.18.cloned.1.call-start = ((), (), s32[]{:S(2)}) async-start(), calls=%async_computation.14 | async-start | bytes 2228224 | tf_op jit(solution)/shard_map/reduce_scatter | solution.py:234
  360.8 445.9 %reduce-scatter.14.cloned.1.call-start = ((), (), s32[]{:S(2)}) async-start(), calls=%async_computation.12 | async-start | bytes 2228224 | tf_op jit(solution)/shard_map/reduce_scatter | solution.py:230
  365.0 506.6 %reduce-scatter.16.cloned.1.call-start = ((), (), s32[]{:S(2)}) async-start(), calls=%async_computation.13 | async-start | bytes 2228224 | tf_op jit(solution)/shard_map/reduce_scatter | solution.py:231
  369.2 587.9 %reduce-scatter.20.cloned.1.call-start = ((), (), s32[]{:S(2)}) async-start(), calls=%async_computation.15 | async-start | bytes 6127616 | tf_op jit(solution)/shard_map/reduce_scatter | solution.py:232
  378.0 664.7 %reduce-scatter.22.cloned.1.call-start = ((), (), s32[]{:S(2)}) async-start(), calls=%async_computation.16 | async-start | bytes 6127616 | tf_op jit(solution)/shard_map/reduce_scatter | solution.py:233
  386.7 741.8 %reduce-scatter.24.cloned.1.call-start = ((), (), s32[]{:S(2)}) async-start(), calls=%async_computation.17 | async-start | bytes 6127616 | tf_op jit(solution)/shard_map/reduce_scatter | solution.py:235
  549.4 579.0 %copy-start.1 = (bf16[1408,1024]{1,0:T(8,128)(2,1)S(1)}, bf16[1408,1024]{1,0:T(8,128)(2,1)}, u32[]{:S(2)}) copy-start(bf16[1408,1024]{1,0:T(8,128)(2,1)} %param.24) | copy-start | bytes 8650756
  (45 other events, 115.3 us)
Sparse Core Ops, SparseCore 0:
  47.8 109.6 all-reduce.5
  188.2 107.8 all-reduce.7
  346.8 198.5 all-reduce.9
  549.5 61.8 reduce-scatter.11
  616.0 60.5 reduce-scatter.9
  680.8 60.4 reduce-scatter.17
  746.1 60.5 reduce-scatter.13
  811.0 60.5 reduce-scatter.15
  876.5 80.5 reduce-scatter.19
  962.0 80.6 reduce-scatter.21
  1047.7 80.7 reduce-scatter.23
where the time goes:
time: 1140 us
  waiting for transfers between devices  898 us (79%)
  matrix products  126 us (11%)
  blocking collectives  42.7 us (4%)
  other arithmetic  32.2 us (3%)
  local copies, waits for them, and re-layouts  19.3 us (2%)
  between operations  15.6 us (1%)
    psum x3, waiting for transfers between devices, tensor_sum(): return lax.psum(values, 'tensor')  326 us
    reduce_scatter x1, waiting for transfers between devices, local(): lax.psum_scatter(down_grad, 'dp', scatter_dimension=1, tiled=True)  85.7 us
    reduce_scatter x1, waiting for transfers between devices, local(): lax.psum_scatter(left_grad, 'dp', scatter_dimension=0, tiled=True)  85.6 us
    reduce_scatter x1, waiting for transfers between devices, local(): lax.psum_scatter(right_grad, 'dp', scatter_dimension=0, tiled=True)  85.5 us
    reduce_scatter x1, waiting for transfers between devices, local(): lax.psum_scatter(value_grad, 'dp', scatter_dimension=0, tiled=True)  65.3 us
    reduce_scatter x1, waiting for transfers between devices, local(): lax.psum_scatter(query_grad, 'dp', scatter_dimension=0, tiled=True)  65.2 us
    reduce_scatter x1, waiting for transfers between devices, local(): lax.psum_scatter(gate_grad, 'dp', scatter_dimension=0, tiled=True)  64.9 us
    reduce_scatter x1, waiting for transfers between devices, local(): lax.psum_scatter(output_grad, 'dp', scatter_dimension=1, tiled=True)  64.7 us
  transfers between devices with their start and end apart: 11, of which 11 were waited for; matrix products, arithmetic and copies ran while one was open for 6% of the time, Pallas kernels for 0%

commit v1 on v0

--- a/solution.py
+++ b/solution.py
@@ -37,12 +37,27 @@
     return sigma * (1.0 + values * (1.0 - sigma))
 
 
-def tensor_sum(values):
-    return lax.psum(values, "tensor")
+def swap_half(values):
+    return lax.ppermute(values, "tensor", [(0, 1), (1, 0)])
+
+
+def sum_half(values, side):
+    half = values.shape[0] // 2
+    halves = values.reshape(2, half, values.shape[1])
+    other = lax.dynamic_index_in_dim(halves, 1 - side, 0, keepdims=False).astype(jnp.bfloat16)
+    own = lax.dynamic_index_in_dim(halves, side, 0, keepdims=False)
+    return own + swap_half(other).astype(jnp.float32)
+
+
+def join_halves(own, side):
+    other = swap_half(own)
+    first = jnp.where(side == 0, own, other)
+    second = jnp.where(side == 0, other, own)
+    return jnp.concatenate([first, second], axis=0)
 
 
 def row_stat(values):
-    return lax.psum(values, "tensor")
+    return values + lax.ppermute(values, "tensor", [(0, 1), (1, 0)])
 
 
 def decay_mask(segment, decays, offset, height):
@@ -157,27 +172,37 @@
     normed_heads = heads_out * scale_out
     scaled_heads = normed_heads * gain_flat
     mixed = (scaled_heads * gate_act).astype(jnp.bfloat16)
+    side = lax.axis_index("tensor")
+    half_rows = rows_total // 2
+
+    def own_half(values):
+        return lax.dynamic_slice_in_dim(values, side * half_rows, half_rows, 0)
+
     attn_part = product(mixed, output_weight)
-    hidden = source + tensor_sum(attn_part)
+    hidden = own_half(tokens).astype(jnp.float32) + sum_half(attn_part, side)
     scale_mid = rms_scale(hidden)
-    lifted = (hidden * scale_mid).astype(jnp.bfloat16)
+    lifted_own = (hidden * scale_mid).astype(jnp.bfloat16)
+    lifted = join_halves(lifted_own, side)
     left_act = product(lifted, left_weight)
     right_act = product(lifted, right_weight)
     joined = (left_act * right_act).astype(jnp.bfloat16)
-    down_part = product(joined, down_weight)
-    block_out = (hidden + tensor_sum(down_part)).astype(jnp.bfloat16)
     grad_joined = product_nt(cotangent, down_weight)
-    down_grad = product_tn(joined, cotangent)
     grad_left = (grad_joined * right_act).astype(jnp.bfloat16)
     grad_right = (grad_joined * left_act).astype(jnp.bfloat16)
+    lifted_part = product_nt(grad_left, left_weight) + product_nt(grad_right, right_weight)
+    grad_lifted = sum_half(lifted_part, side)
+    down_part = product(joined, down_weight)
+    block_out = join_halves((hidden + sum_half(down_part, side)).astype(jnp.bfloat16), side)
+    down_grad = product_tn(cotangent, joined)
     left_grad = product_tn(lifted, grad_left)
     right_grad = product_tn(lifted, grad_right)
-    lifted_part = product_nt(grad_left, left_weight) + product_nt(grad_right, right_weight)
-    grad_hidden = cotangent.astype(jnp.float32) + rms_back(
-        hidden, scale_mid, tensor_sum(lifted_part)
-    )
-    grad_low = grad_hidden.astype(jnp.bfloat16)
-    output_grad = product_tn(mixed, grad_low)
+    ffn_total = lax.psum_scatter(
+        jnp.concatenate([left_grad, right_grad, down_grad], axis=1).astype(jnp.bfloat16),
+        "dp", scatter_dimension=0, tiled=True,
+    ).astype(jnp.float32)
+    grad_hidden = own_half(cotangent).astype(jnp.float32) + rms_back(hidden, scale_mid, grad_lifted)
+    grad_low = join_halves(grad_hidden.astype(jnp.bfloat16), side)
+    output_grad = product_tn(grad_low, mixed)
     grad_mixed = product_nt(grad_low, output_weight)
     grad_scaled = grad_mixed * gate_act
     grad_gate = (grad_mixed * scaled_heads).astype(jnp.bfloat16)
@@ -213,28 +238,27 @@
         + product_nt(value_pull, value_weight)
         + product_nt(grad_gate, gate_weight)
     )
-    tokens_grad = grad_hidden + rms_back(source, scale_in, tensor_sum(normed_part))
-    (
-        query_total,
-        key_total,
-        value_total,
-        gate_total,
-        left_total,
-        right_total,
-        output_total,
-        down_total,
-        gain_total,
-    ) = (
-        lax.psum_scatter(query_grad, "dp", scatter_dimension=0, tiled=True),
-        lax.psum_scatter(key_grad, "dp", scatter_dimension=0, tiled=True),
-        lax.psum_scatter(value_grad, "dp", scatter_dimension=0, tiled=True),
-        lax.psum_scatter(gate_grad, "dp", scatter_dimension=0, tiled=True),
-        lax.psum_scatter(left_grad, "dp", scatter_dimension=0, tiled=True),
-        lax.psum_scatter(right_grad, "dp", scatter_dimension=0, tiled=True),
-        lax.psum_scatter(output_grad, "dp", scatter_dimension=1, tiled=True),
-        lax.psum_scatter(down_grad, "dp", scatter_dimension=1, tiled=True),
-        lax.psum_scatter(gain_grad, "dp", scatter_dimension=1, tiled=True),
-    )
+    tokens_own = grad_hidden + rms_back(own_half(source), own_half(scale_in), sum_half(normed_part, side))
+    tokens_grad = join_halves(tokens_own.astype(jnp.bfloat16), side).astype(jnp.float32)
+    dp = lax.axis_size("dp")
+    gain_rows = gain_grad.reshape(local_heads, dp, head_size // dp).transpose(1, 0, 2).reshape(dp, -1)
+    gain_rows = jnp.pad(gain_rows, ((0, 0), (0, query_grad.shape[0] // dp - gain_rows.shape[1])))
+    gain_block = jnp.pad(gain_rows.reshape(-1, 1), ((0, 0), (0, 127)))
+    attn_total = lax.psum_scatter(
+        jnp.concatenate(
+            [query_grad, key_grad, value_grad, gate_grad, output_grad, gain_block], axis=1
+        ).astype(jnp.bfloat16),
+        "dp", scatter_dimension=0, tiled=True,
+    ).astype(jnp.float32)
+    query_total, key_total, value_total, gate_total, output_turned = (
+        attn_total[:, at * inner_width : (at + 1) * inner_width] for at in range(5)
+    )
+    output_total = output_turned.T
+    width = head_size // dp
+    gain_total = attn_total[: local_heads * width, 5 * inner_width].reshape(local_heads, width)
+    units = left_weight.shape[1]
+    left_total, right_total = ffn_total[:, :units], ffn_total[:, units : 2 * units]
+    down_total = ffn_total[:, 2 * units :].T
     return (
         block_out,
         tokens_grad,

time: 1140 us -> 449 us (0.39)
  waiting for transfers between devices: 898 us -> 248 us
  blocking collectives: 42.7 us -> 0 us
  matrix products: 126 us -> 100 us
  local copies, waits for them, and re-layouts: 19.3 us -> 33.3 us
  starting transfers between devices: 1.33 us -> 14.5 us
    reduce_scatter x8 -> x1, waiting for transfers between devices: 572 us -> 89.8 us  [local(): lax.psum_scatter(jnp.concatenate([left_grad, right_grad, down_grad], axis...]
    psum x3 -> x0, waiting for transfers between devices: 326 us -> none  [tensor_sum(): return lax.psum(values, 'tensor')]
    ppermute x0 -> x10, waiting for transfers between devices: none -> 158 us  [the longest x8 155 us: swap_half(): return lax.ppermute(values, 'tensor', [(0, 1), (1, 0)])]
    unnamed x1 -> x0, blocking collectives: 31.7 us -> none
    dot_general x8, matrix products: 47.6 us -> 25.2 us  [product_tn(): lax.dot_general(left_op, right_op, (((0,), (0,)), ((), ())), preferred_el...]
    ppermute x0 -> x10, starting transfers between devices: none -> 14.2 us  [the longest x8 10.3 us: swap_half(): return lax.ppermute(values, 'tensor', [(0, 1), (1, 0)])]
    unnamed x118 -> x146, local copies, waits for them, and re-layouts: 19.2 us -> 26.8 us
  transfers between devices with their start and end apart: 11 -> 12, of which waited for: 11 -> 11; matrix products, arithmetic and copies ran while one was open for 6% -> 11% of each run, Pallas kernels for 0% -> 0%
where the time goes in v1:
time: 449 us; the launch traced here: 441 us
  waiting for transfers between devices  248 us (55%)
  matrix products  100 us (22%)
  local copies, waits for them, and re-layouts  33.3 us (7%)
  other arithmetic  29.6 us (7%)
  between operations  15.4 us (3%)
  starting transfers between devices  14.5 us (3%)
    ppermute x8, waiting for transfers between devices, swap_half(): return lax.ppermute(values, 'tensor', [(0, 1), (1, 0)])  155 us
    reduce_scatter x1, waiting for transfers between devices, local(): lax.psum_scatter(jnp.concatenate([left_grad, right_grad, down_grad], axis...  89.8 us
    dot_general x8, matrix products, product(): return jnp.dot(left_op, right_op, preferred_element_type=jnp.float32)  27.9 us
    unnamed x146, local copies, waits for them, and re-layouts  26.8 us
    dot_general x8, matrix products, product_nt(): lax.dot_general(left_op, right_op, (((1,), (1,)), ((), ())), preferred_el...  26.4 us
    dot_general x8, matrix products, product_tn(): lax.dot_general(left_op, right_op, (((0,), (0,)), ((), ())), preferred_el...  25.2 us
    ppermute x8, starting transfers between devices, swap_half(): return lax.ppermute(values, 'tensor', [(0, 1), (1, 0)])  10.3 us
  transfers between devices with their start and end apart: 12, of which 11 were waited for; matrix products, arithmetic and copies ran while one was open for 11% of the time, Pallas kernels for 0%

profile of v1, /device:TPU:0, one launch (start us, length us, event | category | flops | bytes accessed | tf_op | source)
XLA Modules:
  0.0 441.5 jit_solution(12278835552995644547)
XLA Ops:
  37.2 5.4 %multiply_convert_fusion.10 = (bf16[1024,512]{0,1:T(8,128)(2,1)S(1)}, f32[1024,512]{0,1:T(8,128)}) fusion(f32[1024,4,128]{0,2,1:T(8,128)} %get-tuple-element.117, f32[512]{0:T(512)S(1)} %bitcast_convert_fusion, f32[1024]{0:T(1024)S(1)} %get-tuple-element.98, bf16[1024,512]{1,0:T(8,128)(2,1)} %param.19, f32[1024]{0:T(1024)S(1)} %add_rsqrt_fusion.1, ...), kind=kOutput, calls=%fused_computation.54 | convolution fusion | flops 1078984704 | bytes 8398848 | tf_op jit(solution)/shard_map/dot_general | solution.py:10
  49.2 22.3 %collective-permute-done.1 = bf16[512,1024]{1,0:T(8,128)(2,1)} collective-permute-done((bf16[512,1024]{1,0:T(8,128)(2,1)}, bf16[512,1024]{1,0:T(8,128)(2,1)}, u32[]{:S(2)}, u32[]{:S(2)}) %collective-permute-start.1) | collective-permute-done | bytes 1048608 | tf_op jit(solution)/shard_map/ppermute | solution.py:41
  78.5 6.0 %fusion.41 = f32[1024,1408]{1,0:T(8,128)S(1)} fusion(bf16[1024,1024]{1,0:T(8,128)(2,1)} %param.25, bf16[1408,1024]{1,0:T(8,128)(2,1)} %param.24), kind=kOutput, calls=%fused_computation.129 | convolution fusion | flops 2952790016 | bytes 10747904 | tf_op jit(solution)/shard_map/dot_general | solution.py:20
  84.5 15.6 %collective-permute-done.2 = bf16[512,1024]{1,0:T(8,128)(2,1)} collective-permute-done((bf16[512,1024]{1,0:T(8,128)(2,1)}, bf16[512,1024]{1,0:T(8,128)(2,1)}, u32[]{:S(2)}, u32[]{:S(2)}) %collective-permute-start.2) | collective-permute-done | bytes 1048608 | tf_op jit(solution)/shard_map/ppermute | solution.py:41
  101.7 3.4 fusion.27
  105.2 7.0 %multiply_convert_fusion.4 = (bf16[1024,1408]{1,0:T(8,128)(2,1)}, bf16[1024,1408]{1,0:T(8,128)(2,1)S(1)}, bf16[1024,1408]{1,0:T(8,128)(2,1)}) fusion(f32[1024,1408]{1,0:T(8,128)S(1)} %fusion.41, f32[1024,1408]{1,0:T(8,128)S(1)} %fusion.27, bf16[1024,1408]{1,0:T(8,128)(2,1)S(1)} %copy-done, bf16[512,1024]{1,0:T(8,128)(2,1)S(1)} %get-tuple-element.115, ...), kind=kOutput, calls=%fused_computation.7 | convolution fusion | flops 2965635072 | bytes 25165824 | tf_op jit(solution)/shard_map/dot_general | solution.py:10
  112.2 6.3 %fusion.42 = f32[1024,1024]{1,0:T(8,128)S(1)} fusion(bf16[1024,1408]{1,0:T(8,128)(2,1)} %get-tuple-element.105, bf16[1024,1408]{1,0:T(8,128)(2,1)S(1)} %copy-done), kind=kOutput, calls=%fused_computation.130 | convolution fusion | flops 2952790016 | bytes 9961472 | tf_op jit(solution)/shard_map/dot_general | solution.py:20
  118.6 3.4 convolution_add_fusion
  123.7 3.4 fusion.40
  128.0 20.4 %collective-permute-done.5 = bf16[512,1024]{1,0:T(8,128)(2,1)S(1)} collective-permute-done((bf16[512,1024]{1,0:T(8,128)(2,1)S(1)}, bf16[512,1024]{1,0:T(8,128)(2,1)S(1)}, u32[]{:S(2)}, u32[]{:S(2)}) %collective-permute-start.5) | collective-permute-done | bytes 1048608 | tf_op jit(solution)/shard_map/ppermute | solution.py:41
  148.8 18.1 %collective-permute-done.3 = bf16[512,1024]{1,0:T(8,128)(2,1)S(1)} collective-permute-done((bf16[512,1024]{1,0:T(8,128)(2,1)S(1)}, bf16[512,1024]{1,0:T(8,128)(2,1)S(1)}, u32[]{:S(2)}, u32[]{:S(2)}) %collective-permute-start.3) | collective-permute-done | bytes 1048608 | tf_op jit(solution)/shard_map/ppermute | solution.py:41
  170.7 20.1 %collective-permute-done.6 = bf16[512,1024]{1,0:T(8,128)(2,1)S(1)} collective-permute-done((bf16[512,1024]{1,0:T(8,128)(2,1)S(1)}, bf16[512,1024]{1,0:T(8,128)(2,1)S(1)}, u32[]{:S(2)}, u32[]{:S(2)}) %collective-permute-start.6) | collective-permute-done | bytes 1048608 | tf_op jit(solution)/shard_map/ppermute | solution.py:41
  191.1 3.4 multiply_reduce_fusion.1
  198.2 3.1 fusion.8
  232.2 8.1 %copy.79 = bf16[1024,2688]{1,0:T(8,128)(2,1)} copy(bf16[1024,2688]{0,1:T(8,128)(2,1)} %pad_dynamic-update-slice_fusion) | data formatting | bytes 11010048
  240.5 6.1 %convolution_convert_fusion.1 = bf16[1024,1408]{1,0:T(8,128)(2,1)S(1)} fusion(bf16[1024,1408]{1,0:T(8,128)(2,1)} %get-tuple-element.103, bf16[512,1024]{1,0:T(8,128)(2,1)} %copy-done.18, bf16[512,1024]{1,0:T(8,128)(2,1)} %copy-done.16), kind=kOutput, calls=%fused_computation.14 | convolution fusion | flops 2958426112 | bytes 7864320 | tf_op jit(solution)/shard_map/dot_general | solution.py:14
  246.6 3.7 convolution_convert_fusion.2
  250.4 3.7 fusion
  254.1 4.1 pad_maximum_fusion
  258.3 3.1 fusion.47
  268.9 23.5 %collective-permute-done.8 = bf16[512,1024]{1,0:T(8,128)(2,1)S(1)} collective-permute-done((bf16[512,1024]{1,0:T(8,128)(2,1)S(1)}, bf16[512,1024]{1,0:T(8,128)(2,1)S(1)}, u32[]{:S(2)}, u32[]{:S(2)}) %collective-permute-start.8) | collective-permute-done | bytes 1048608 | tf_op jit(solution)/shard_map/ppermute | solution.py:41
  294.3 20.5 %collective-permute-done.4 = bf16[512,1024]{1,0:T(8,128)(2,1)S(1)} collective-permute-done((bf16[512,1024]{1,0:T(8,128)(2,1)S(1)}, bf16[512,1024]{1,0:T(8,128)(2,1)S(1)}, u32[]{:S(2)}, u32[]{:S(2)}) %collective-permute-start.4) | collective-permute-done | bytes 1048608 | tf_op jit(solution)/shard_map/ppermute | solution.py:41
  316.4 14.1 %collective-permute-done.9 = bf16[512,1024]{1,0:T(8,128)(2,1)S(1)} collective-permute-done((bf16[512,1024]{1,0:T(8,128)(2,1)S(1)}, bf16[512,1024]{1,0:T(8,128)(2,1)S(1)}, u32[]{:S(2)}, u32[]{:S(2)}) %collective-permute-start.9) | collective-permute-done | bytes 1048608 | tf_op jit(solution)/shard_map/ppermute | solution.py:41
  342.1 89.8 %reduce-scatter.5.cloned.1.call-done = bf16[64,4224]{1,0:T(8,128)(2,1)} async-done(((bf16[1024,4224]{1,0:T(8,128)(2,1)}), bf16[64,4224]{1,0:T(8,128)(2,1)}) %reduce-scatter.5.cloned.1.call-update) | async-done | bytes 540688 | tf_op jit(solution)/shard_map/reduce_scatter | solution.py:199
  (237 shorter events, 111.3 us)
Async XLA Ops:
  7.2 98.0 %copy-start = (bf16[1024,1408]{1,0:T(8,128)(2,1)S(1)}, bf16[1024,1408]{1,0:T(8,128)(2,1)}, u32[]{:S(2)}) copy-start(bf16[1024,1408]{1,0:T(8,128)(2,1)} %param.22) | copy-start | bytes 8650756
  7.2 326.0 %reduce-scatter.7.cloned.1.call-start = ((), (), s32[]{:S(2)}) async-start(), calls=%async_computation.3 | async-start | bytes 5849088
  9.0 17.0 %copy-start.38 = (f32[512,1024]{1,0:T(8,128)}, f32[512,1024]{1,0:T(8,128)S(1)}, u32[]{:S(2)}) copy-start(f32[512,1024]{1,0:T(8,128)S(1)} %maximum_convert_fusion.2) | copy-start | bytes 6291460
  12.5 16.5 %copy-start.21 = (bf16[1024,512]{0,1:T(8,128)(2,1)}, bf16[1024,512]{0,1:T(8,128)(2,1)S(1)}, u32[]{:S(2)}) copy-start(bf16[1024,512]{0,1:T(8,128)(2,1)S(1)} %convolution_convert_fusion.8) | copy-start | bytes 3145732
  32.7 4.5 %collective-permute-start = (f32[1024]{0:T(1024)S(1)}, f32[1024]{0:T(1024)S(1)}, u32[]{:S(2)}, u32[]{:S(2)}) collective-permute-start(f32[1024]{0:T(1024)S(1)} %get-tuple-element.116), channel_id=1, source_target_pairs={{0,1},{1,0},{2,3},{3,2},{4,5},{5,4},{6,7},{7,6},{8,9},{9,8},{10,11... | collective-permute-start | bytes 12296 | tf_op jit(solution)/shard_map/ppermute | solution.py:60
  47.2 24.3 %collective-permute-start.1 = (bf16[512,1024]{1,0:T(8,128)(2,1)}, bf16[512,1024]{1,0:T(8,128)(2,1)}, u32[]{:S(2)}, u32[]{:S(2)}) collective-permute-start(bf16[512,1024]{1,0:T(8,128)(2,1)} %fusion.21), channel_id=1, source_target_pairs={{0,1},{1,0},{2,3},{3,2},{4,5},{5,4},{6,7},{7,6},{8,9},{9,8},{10,11... | collective-permute-start | bytes 3145736 | tf_op jit(solution)/shard_map/ppermute | solution.py:41
  76.7 23.4 %collective-permute-start.2 = (bf16[512,1024]{1,0:T(8,128)(2,1)}, bf16[512,1024]{1,0:T(8,128)(2,1)}, u32[]{:S(2)}, u32[]{:S(2)}) collective-permute-start(bf16[512,1024]{1,0:T(8,128)(2,1)} %multiply_convert_fusion.9), channel_id=1, source_target_pairs={{0,1},{1,0},{2,3},{3,2},{4,5},{5,4},{6,7},{7,6},{8,9},{9,8},{10,11... | collective-permute-start | bytes 3145736 | tf_op jit(solution)/shard_map/ppermute | solution.py:41
  78.5 21.7 %copy-start.3 = (f32[512,1024]{1,0:T(8,128)S(1)}, f32[512,1024]{1,0:T(8,128)}, u32[]{:S(2)}) copy-start(f32[512,1024]{1,0:T(8,128)} %copy-done.2) | copy-start | bytes 6291460
  84.5 17.2 %copy-start.60 = (bf16[1024,1408]{1,0:T(8,128)(2,1)S(1)}, bf16[1024,1408]{1,0:T(8,128)(2,1)}, u32[]{:S(2)}) copy-start(bf16[1024,1408]{1,0:T(8,128)(2,1)} %param.23) | copy-start | bytes 8650756
  112.2 11.6 %copy-start.29 = (bf16[1024,1408]{1,0:T(8,128)(2,1)}, bf16[1024,1408]{1,0:T(8,128)(2,1)S(1)}, u32[]{:S(2)}) copy-start(bf16[1024,1408]{1,0:T(8,128)(2,1)S(1)} %get-tuple-element.104) | copy-start | bytes 8650756
  122.2 26.2 %collective-permute-start.5 = (bf16[512,1024]{1,0:T(8,128)(2,1)S(1)}, bf16[512,1024]{1,0:T(8,128)(2,1)S(1)}, u32[]{:S(2)}, u32[]{:S(2)}) collective-permute-start(bf16[512,1024]{1,0:T(8,128)(2,1)S(1)} %fusion.23), channel_id=1, source_target_pairs={{0,1},{1,0},{2,3},{3,2},{4,5},{5,4},{6,7},{7,6},{8,9},{9,8},{10,11... | collective-permute-start | bytes 3145736 | tf_op jit(solution)/shard_map/ppermute | solution.py:41
  127.3 39.6 %copy-start.56 = (bf16[1024,1024]{1,0:T(8,128)(2,1)S(1)}, bf16[1024,1024]{1,0:T(8,128)(2,1)}, u32[]{:S(2)}) copy-start(bf16[1024,1024]{1,0:T(8,128)(2,1)} %param.25) | copy-start | bytes 6291460
  127.3 39.6 %collective-permute-start.3 = (bf16[512,1024]{1,0:T(8,128)(2,1)S(1)}, bf16[512,1024]{1,0:T(8,128)(2,1)S(1)}, u32[]{:S(2)}, u32[]{:S(2)}) collective-permute-start(bf16[512,1024]{1,0:T(8,128)(2,1)S(1)} %fusion.22), channel_id=1, source_target_pairs={{0,1},{1,0},{2,3},{3,2},{4,5},{5,4},{6,7},{7,6},{8,9},{9,8},{10,11... | collective-permute-start | bytes 3145736 | tf_op jit(solution)/shard_map/ppermute | solution.py:41
  166.9 24.1 %copy-start.51 = (bf16[512,1024]{1,0:T(8,128)(2,1)S(1)}, bf16[512,1024]{1,0:T(8,128)(2,1)}, u32[]{:S(2)}) copy-start(bf16[512,1024]{1,0:T(8,128)(2,1)} %param.20) | copy-start | bytes 3145732
  169.5 21.6 %copy-start.10 = (f32[1024,4,128]{0,2,1:T(8,128)S(1)}, f32[1024,4,128]{0,2,1:T(8,128)}, u32[]{:S(2)}) copy-start(f32[1024,4,128]{0,2,1:T(8,128)} %get-tuple-element.117) | copy-start | bytes 6291460
  169.5 21.6 %copy-start.13 = (f32[1024,512]{0,1:T(8,128)S(1)}, f32[1024,512]{0,1:T(8,128)}, u32[]{:S(2)}) copy-start(f32[1024,512]{0,1:T(8,128)} %get-tuple-element.139) | copy-start | bytes 6291460
  169.5 21.3 %collective-permute-start.6 = (bf16[512,1024]{1,0:T(8,128)(2,1)S(1)}, bf16[512,1024]{1,0:T(8,128)(2,1)S(1)}, u32[]{:S(2)}, u32[]{:S(2)}) collective-permute-start(bf16[512,1024]{1,0:T(8,128)(2,1)S(1)} %get-tuple-element.99), channel_id=1, source_target_pairs={{0,1},{1,0},{2,3},{3,2},{4,5},{5,4},{6,7},{7,6},{8,9},{9,8},{10,11... | collective-permute-start | bytes 3145736 | tf_op jit(solution)/shard_map/ppermute | solution.py:41
  194.5 3.7 collective-permute-start.7
  240.2 191.7 %reduce-scatter.5.cloned.1.call-start = ((), (), s32[]{:S(2)}) async-start(), calls=%async_computation.2 | async-start | bytes 9191424 | tf_op jit(solution)/shard_map/reduce_scatter | solution.py:199
  266.2 26.2 %collective-permute-start.8 = (bf16[512,1024]{1,0:T(8,128)(2,1)S(1)}, bf16[512,1024]{1,0:T(8,128)(2,1)S(1)}, u32[]{:S(2)}, u32[]{:S(2)}) collective-permute-start(bf16[512,1024]{1,0:T(8,128)(2,1)S(1)} %fusion.24), channel_id=1, source_target_pairs={{0,1},{1,0},{2,3},{3,2},{4,5},{5,4},{6,7},{7,6},{8,9},{9,8},{10,11... | collective-permute-start | bytes 3145736 | tf_op jit(solution)/shard_map/ppermute | solution.py:41
  267.7 24.9 %copy-start.12 = (f32[512,1024]{1,0:T(8,128)S(1)}, f32[512,1024]{1,0:T(8,128)}, u32[]{:S(2)}) copy-start(f32[512,1024]{1,0:T(8,128)} %get-tuple-element.100) | copy-start | bytes 6291460
  267.7 47.1 %collective-permute-start.4 = (bf16[512,1024]{1,0:T(8,128)(2,1)S(1)}, bf16[512,1024]{1,0:T(8,128)(2,1)S(1)}, u32[]{:S(2)}, u32[]{:S(2)}) collective-permute-start(bf16[512,1024]{1,0:T(8,128)(2,1)S(1)} %copy-done.25), channel_id=1, source_target_pairs={{0,1},{1,0},{2,3},{3,2},{4,5},{5,4},{6,7},{7,6},{8,9},{9,8},{10,11... | collective-permute-start | bytes 3145736 | tf_op jit(solution)/shard_map/ppermute | solution.py:41
  293.3 37.2 %collective-permute-start.9 = (bf16[512,1024]{1,0:T(8,128)(2,1)S(1)}, bf16[512,1024]{1,0:T(8,128)(2,1)S(1)}, u32[]{:S(2)}, u32[]{:S(2)}) collective-permute-start(bf16[512,1024]{1,0:T(8,128)(2,1)S(1)} %add_convert_fusion), channel_id=1, source_target_pairs={{0,1},{1,0},{2,3},{3,2},{4,5},{5,4},{6,7},{7,6},{8,9},{9,8},{10,11... | collective-permute-start | bytes 3145736 | tf_op jit(solution)/shard_map/ppermute | solution.py:41
  338.9 95.3 %copy-start.1 = (bf16[1024,1408]{1,0:T(8,128)(2,1)S(1)}, bf16[1024,1408]{1,0:T(8,128)(2,1)}, u32[]{:S(2)}) copy-start(bf16[1024,1408]{1,0:T(8,128)(2,1)} %param.22) | copy-start | bytes 8650756
  (57 other events, 183.6 us)
Sparse Core Ops, SparseCore 0:
  240.3 80.6 reduce-scatter.6
  325.7 106.2 reduce-scatter.4

commit v2 on v0

v2 whole, which is shorter than its diff:
```python
import functools

import jax
import jax.numpy as jnp
from jax import lax
from jax.experimental import pallas as pl
from jax.experimental.pallas import tpu as pltpu
from jax.sharding import PartitionSpec as P

MESH = pl.DeviceIdType.MESH
eps = 1e-06
BAND = 384
BLOCK = 256
SPAN = BAND + BLOCK
F32 = jnp.float32
BF16 = jnp.bfloat16
VMEM_LIMIT = 62 * 1024 * 1024


def nn(left_op, right_op):
    return jnp.dot(left_op, right_op, preferred_element_type=F32)


def nt(left_op, right_op):
    return lax.dot_general(
        left_op, right_op, (((1,), (1,)), ((), ())), preferred_element_type=F32
    )


def at(start):
    return pl.ds(pl.multiple_of(start, BLOCK), BLOCK)


def rms_scale(values):
    return lax.rsqrt(jnp.mean(values * values, axis=1, keepdims=True) + eps)


def rms_back(values, scale, grads):
    return scale * grads - values * (scale * scale * scale) * jnp.mean(
        values * grads, axis=1, keepdims=True
    )


def eye():
    shape = (128, 128)
    return lax.broadcasted_iota(jnp.int32, shape, 0) == lax.broadcasted_iota(jnp.int32, shape, 1)


def to_column(rows):
    parts = [
        jnp.sum(jnp.where(eye(), rows[i : i + 1, :], 0.0), axis=1, keepdims=True)
        for i in range(rows.shape[0])
    ]
    return jnp.concatenate(parts, axis=0)


def to_rows(column):
    parts = [
        jnp.sum(jnp.where(eye(), column[i : i + 128, :], 0.0), axis=0, keepdims=True)
        for i in range(0, column.shape[0], 128)
    ]
    return jnp.concatenate(parts, axis=0)


def iota_f32(shape, axis):
    return lax.broadcasted_iota(jnp.int32, shape, axis).astype(F32)


def attend(
    seg_ref, decay_ref, tok_ref, wq_ref, wk_ref, wv_ref, wg_ref, gain_ref,
    u_ref, heads_ref, gate_ref, q_ref, k_ref, v_ref, sq_ref, sk_ref, sums_ref,
    k_all, v_all,
):
    step = pl.program_id(0)
    width = q_ref.shape[1]

    @pl.when(step == 0)
    def _():
        k_all[:BAND, :] = jnp.zeros((BAND, width), BF16)
        v_all[:BAND, :] = jnp.zeros((BAND, width), BF16)

    source = tok_ref[...].astype(F32)
    normed = (source * rms_scale(source)).astype(BF16)
    pre = nn(normed, wk_ref[...])
    sigma = jax.nn.sigmoid(pre)
    key_rows = (pre * sigma).astype(BF16)
    sk_ref[...] = (sigma * (1.0 + pre * (1.0 - sigma))).astype(BF16)
    k_ref[...] = key_rows
    here = pl.ds(pl.multiple_of(BAND + step * BLOCK, 128), BLOCK)
    k_all[here, :] = key_rows
    value_rows = nn(normed, wv_ref[...]).astype(BF16)
    v_ref[...] = value_rows
    v_all[here, :] = value_rows
    pre = nn(normed, wq_ref[...])
    sigma = jax.nn.sigmoid(pre)
    queries = (pre * sigma).astype(BF16)
    sq_ref[...] = (sigma * (1.0 + pre * (1.0 - sigma))).astype(BF16)
    q_ref[...] = queries
    gate = nn(normed, wg_ref[...])
    gate_ref[...] = gate.astype(BF16)

    span = pl.ds(pl.multiple_of(step * BLOCK, BLOCK), SPAN)
    seg_keys = seg_ref[0:1, span]
    seg_rows = to_column(
        jnp.concatenate(
            [
                seg_ref[0:1, pl.ds(pl.multiple_of(BAND + step * BLOCK + i, 128), 128)]
                for i in range(0, BLOCK, 128)
            ],
            axis=0,
        )
    )
    row_at = iota_f32((BLOCK, 1), 0)
    key_at = iota_f32((1, SPAN), 1) - float(BAND)
    allowed = (seg_rows == seg_keys) & (row_at >= key_at)
    total = jnp.zeros((BLOCK, 1), F32)
    for head in range(width // 128):
        lanes = slice(head * 128, head * 128 + 128)
        decay = decay_ref[head]
        scores = nt(queries[:, lanes], k_all[span, lanes])
        falloff = jnp.exp(-decay * row_at) * jnp.exp(decay * key_at)
        weighted = jnp.where(allowed, scores * falloff, 0.0).astype(BF16)
        heads = nn(weighted, v_all[span, lanes])
        total = total + jnp.sum(heads * heads, axis=1, keepdims=True)
        heads_ref[:, lanes] = heads.astype(BF16)
        u_ref[:, lanes] = (heads * gain_ref[0:1, lanes] * gate[:, lanes]).astype(BF16)
    for part in range(BLOCK // 128):
        sums_ref[pl.ds(step * (BLOCK // 128) + part, 1), :] = to_rows(
            total[part * 128 : part * 128 + 128, :]
        )


def run_attend(segments, decays, tokens, wq, wk, wv, wg, gain):
    rows, features = tokens.shape
    width = wq.shape[1]
    whole = lambda *shape: pl.BlockSpec(shape, lambda i: (0,) * len(shape))
    block = lambda columns: pl.BlockSpec((BLOCK, columns), lambda i: (i, 0))
    return pl.pallas_call(
        attend,
        grid=(rows // BLOCK,),
        in_specs=[
            whole(*segments.shape),
            pl.BlockSpec(memory_space=pltpu.SMEM),
            block(features),
            whole(features, width), whole(features, width), whole(features, width), whole(features, width),
            whole(1, width),
        ],
        out_specs=[block(width)] * 8 + [whole(rows // 128, 128)],
        out_shape=[jax.ShapeDtypeStruct((rows, width), BF16)] * 8
        + [jax.ShapeDtypeStruct((rows // 128, 128), F32)],
        scratch_shapes=[pltpu.VMEM((BAND + rows, width), BF16)] * 2,
        compiler_params=pltpu.CompilerParams(vmem_limit_bytes=VMEM_LIMIT),
        cost_estimate=pl.CostEstimate(flops=6 * 10**9, bytes_accessed=15 * 2**20, transcendentals=10**6),
        name="attend",
    )(segments, decays, tokens, wq, wk, wv, wg, gain)


def tiles(extent, most=512):
    return [(start, min(most, extent - start)) for start in range(0, extent, most)]


def rest(
    ways,
    seg_ref, decay_ref, sums_ref, gain_ref, tok, cot, u, wo, wo_part, wl, wr, wd, wq, wk, wv, wg,
    heads, gate, q, k, v, sq, sk,
    out_ref, tg_ref, ffn_ref, attn_ref, gain_out,
    lifted, u_in, wo_peer, sum_in, back_in, down_in, mixed_grad, cross, norm_in, turn_in,
    ffn_c, ffn_y, ffn_z, att_c, att_y, att_z, gain_in,
    u_own, wo_own, mixed_out, down_out, hidden, grad_hidden, scale_rows, core_out, gain_sum, turn_out,
    send, recv, dp_send, dp_recv, z_send, z_recv, local,
):
    dp, side = lax.axis_index("dp"), lax.axis_index("tensor")
    core, second, third = lax.rem(dp, 2), lax.rem(lax.div(dp, 2), 2), lax.div(dp, 4)
    rows, features = tok.shape
    width = wq.shape[1]
    units = wl.shape[1]
    half = rows // 2
    thirds = ways // 4
    share = features // ways
    full_inner = float(2 * width)
    own0, other0 = side * half, (1 - side) * half
    across = (dp, 1 - side)
    sibling = (dp + 1 - 2 * core, side)
    beside = (dp + 2 - 4 * second, side)

    def far(hop):
        return (lax.rem(third + hop, thirds) * 4 + second * 2 + core, side)

    def remote(source, target, send_sem, recv_sem, device):
        return pltpu.make_async_remote_copy(
            src_ref=source, dst_ref=target, send_sem=send_sem, recv_sem=recv_sem,
            device_id=device, device_id_type=MESH,
        )

    def over_x(index, source, target):
        return remote(source, target, send.at[index], recv.at[index], across)

    def load(index, source, target):
        copy = pltpu.make_async_copy(source, target, local.at[index])
        copy.start()
        return copy

    def put_turned(target, block, column):
        turned = jnp.transpose(block)
        for owner in range(ways):
            place = (owner % 2) * (ways // 2) + (owner // 2 % 2) * (ways // 4) + owner // 4
            target[place * share : (place + 1) * share, column] = turned[
                owner * share : (owner + 1) * share, :
            ]

    def chunk(part):
        return at(part * BLOCK)

    def u_copy(part):
        return over_x(part, u.at[at(other0 + part * BLOCK), :], u_in.at[chunk(part), :])

    def lifted_copy(part):
        place = lifted.at[at(own0 + part * BLOCK), :]
        return over_x(4 + part, place, place)

    def back_copy(source, part):
        return over_x(6 + part, source.at[chunk(part), :], back_in.at[chunk(part), :])

    def mixed_copy(part):
        return over_x(
            8 + part, mixed_out.at[chunk(part), :], mixed_grad.at[at(own0 + part * BLOCK), :]
        )

    def down_copy(part):
        return over_x(11 + part, down_out.at[chunk(part), :], down_in.at[chunk(part), :])

    def norm_copy(source, part):
        return over_x(13 + part, source.at[chunk(part), :], norm_in.at[chunk(part), :])

    def out_copy(source, part):
        return over_x(15 + part, source.at[chunk(part), :], out_ref.at[at(own0 + part * BLOCK), :])

    def tg_copy(source, part):
        return over_x(17 + part, source.at[chunk(part), :], tg_ref.at[at(own0 + part * BLOCK), :])

    def core_copy(first, block, landing, columns):
        return remote(
            core_out.at[:, pl.ds(0, columns)], landing.at[block],
            dp_send.at[0, first + block], dp_recv.at[0, first + block], sibling,
        )

    def second_copy(first, block, summed, landing):
        return remote(
            summed.at[block, at((1 - second) * BLOCK), :], landing.at[block],
            dp_send.at[1, first + block], dp_recv.at[1, first + block], beside,
        )

    def third_copy(first, block, hop, summed, landing):
        piece = pl.ds(pl.multiple_of(lax.rem(third + hop, thirds) * share, share), share)
        return remote(
            summed.at[block, piece, :], landing.at[block, hop - 1],
            z_send.at[first + block, hop - 1], z_recv.at[first + block, hop - 1], far(hop),
        )

    def stage_send(turned, grads, columns, copy):
        def one(part, carry):
            left_op = turned[at((1 - core) * 2 * BLOCK + part * BLOCK), :]
            for start, size in tiles(columns):
                core_out[chunk(part), start : start + size] = nn(
                    left_op, grads[:, start : start + size]
                ).astype(BF16)
            return carry

        lax.fori_loop(0, 2, one, 0)
        copy.start()

    def stage_core(turned, grads, columns, copy, landing, onward):
        copy.wait()

        def one(part, carry):
            left_op = turned[at(core * 2 * BLOCK + part * BLOCK), :]
            for start, size in tiles(columns):
                cut = slice(start, start + size)
                total = nn(left_op, grads[:, cut]) + landing[chunk(part), cut].astype(F32)
                landing[chunk(part), cut] = total.astype(BF16)
            return carry

        lax.fori_loop(0, 2, one, 0)
        onward.start()

    def stage_second(first, block, summed, landing, group_out):
        copy = second_copy(first, block, summed, landing)
        copy.wait()
        for start, size in tiles(landing.shape[2]):
            cut = slice(start, start + size)
            total = (
                summed[block, at(second * BLOCK), cut].astype(F32)
                + landing[block, :, cut].astype(F32)
            )
            landing[block, :, cut] = total.astype(BF16)
        for hop in range(1, thirds):
            third_copy(first, block, hop, landing, group_out).start()

    def stage_third(first, block, summed, landing):
        mine = pl.ds(pl.multiple_of(third * share, share), share)
        total = summed[block, mine, :].astype(F32)
        for hop in range(1, thirds):
            third_copy(first, block, hop, summed, landing).wait()
            total = total + landing[block, hop - 1].astype(F32)
        return total

    def gain_copy(stage, slot, device):
        return remote(
            gain_sum.at[stage], gain_in.at[slot], z_send.at[6, slot], z_recv.at[6, slot], device
        )

    barrier = pltpu.get_barrier_semaphore()
    partners = [across, sibling, beside] + [far(hop) for hop in range(1, thirds)]
    for device in partners:
        pl.semaphore_signal(barrier, inc=1, device_id=device, device_id_type=MESH)
    pl.semaphore_wait(barrier, len(partners))

    def middle(tok_own, cot_all, turned, w_left, w_right, w_down, hidden_units, back_out, low_turned, mixed):
        part_copy = load(1, wo_part, wo_peer.at[at(core * BLOCK), :])
        loads = [
            load(0, wo, wo_own),
            load(2, u.at[pl.ds(pl.multiple_of(own0, BLOCK), half), :], u_own),
            load(3, tok.at[pl.ds(pl.multiple_of(own0, BLOCK), half), :], tok_own),
            load(4, cot, cot_all),
        ]
        weights = [load(5, wl, w_left), load(6, wr, w_right), load(7, wd, w_down)]
        for part in range(2):
            u_copy(part).start()
        sum_copy = over_x(2, sums_ref, sum_in)
        sum_copy.start()
        part_copy.wait()
        quarter = wo_peer.at[at(core * BLOCK), :]
        quarter_copy = remote(quarter, quarter, send.at[3], recv.at[3], sibling)
        quarter_copy.start()
        for copy in loads:
            copy.wait()

        def own_heads(part, carry):
            grad_hidden[chunk(part), :] = nn(u_own[chunk(part), :], wo_own[...])
            return carry

        lax.fori_loop(0, 2, own_heads, 0)

        def turn(part, carry):
            put_turned(turned.at[1], cot_all[chunk(part), :], chunk(part))
            return carry

        lax.fori_loop(0, rows // BLOCK, turn, 0)
        quarter_copy.wait()
        sum_copy.wait()
        scale_rows[...] = lax.rsqrt((sums_ref[...] + sum_in[...]) / full_inner + eps)

        def scale_of(block):
            return to_column(
                jnp.concatenate(
                    [
                        scale_rows[pl.ds(block * (BLOCK // 128) + i, 1), :]
                        for i in range(BLOCK // 128)
                    ],
                    axis=0,
                )
            )

        def open_chunk(part, carry):
            u_copy(part).wait()
            scale = scale_of(side * (half // BLOCK) + part)
            from_peer = u_in[chunk(part), :]
            attn = grad_hidden[chunk(part), :] + nn(from_peer, wo_peer[...])
            state = tok_own[chunk(part), :].astype(F32) + scale * attn
            hidden[chunk(part), :] = state
            lifted[at(own0 + part * BLOCK), :] = (state * rms_scale(state)).astype(BF16)
            lifted_copy(part).start()
            mixed[chunk(part), :width] = (u_own[chunk(part), :].astype(F32) * scale).astype(BF16)
            mixed[chunk(part), width:] = (from_peer.astype(F32) * scale).astype(BF16)
            return carry

        lax.fori_loop(0, 2, open_chunk, 0)
        for copy in weights:
            copy.wait()

        def gated(step, carry):
            part = lax.rem(step, 2)
            place = at((side + lax.div(step, 2) * (1 - 2 * side)) * half + part * BLOCK)

            @pl.when(step >= 2)
            def _():
                lifted_copy(part).wait()

            rows_in = lifted[place, :]
            rows_cot = cot_all[place, :]
            for start, size in tiles(units):
                cut = slice(start, start + size)
                left = nn(rows_in, w_left[:, cut])
                right = nn(rows_in, w_right[:, cut])
                grad = nt(rows_cot, w_down[cut, :])
                hidden_units[2, place, cut] = (left * right).astype(BF16)
                hidden_units[0, place, cut] = (grad * right).astype(BF16)
                hidden_units[1, place, cut] = (grad * left).astype(BF16)
            back = nt(hidden_units[0, place, :], w_left[...]) + nt(
                hidden_units[1, place, :], w_right[...]
            )

            @pl.when(step < 2)
            def _():
                grad_hidden[chunk(part), :] = back

            @pl.when(step >= 2)
            def _():
                back_out[chunk(part), :] = back.astype(BF16)
                back_copy(back_out, part).start()

            put_turned(turned.at[0], rows_in, place)
            return carry

        lax.fori_loop(0, 4, gated, 0)

        def down_other(part, carry):
            down_out[chunk(part), :] = nn(
                hidden_units[2, at(other0 + part * BLOCK), :], w_down[...]
            ).astype(BF16)
            return carry

        lax.fori_loop(0, 2, down_other, 0)

        def block_step(block, carry):
            lhs, rhs = turned.at[lax.div(block, 2)], hidden_units.at[block]
            first = core_copy(0, block, ffn_c, units)
            stage_send(lhs, rhs, units, first)

            @pl.when(block < 2)
            def _():
                part = block
                back_copy(back_out, part).wait()
                state = hidden[chunk(part), :]
                pulled = grad_hidden[chunk(part), :] + back_in[chunk(part), :].astype(F32)
                grad = cot_all[at(own0 + part * BLOCK), :].astype(F32) + rms_back(
                    state, rms_scale(state), pulled
                )
                grad_hidden[chunk(part), :] = grad
                low = grad.astype(BF16)
                for_own = nt(low, wo_own[...])
                for_peer = nt(low, wo_peer[...])
                mixed_out[chunk(part), :] = for_peer.astype(BF16)
                mixed_grad[at(own0 + part * BLOCK), :] = for_own.astype(BF16)
                mixed_copy(part).start()
                both = jnp.sum(
                    u_own[chunk(part), :].astype(F32) * for_own
                    + u_in[chunk(part), :].astype(F32) * for_peer,
                    axis=1,
                    keepdims=True,
                )
                lanes = to_rows(both)
                for i in range(BLOCK // 128):
                    cross[side, pl.ds(part * (BLOCK // 128) + i, 1), :] = lanes[i : i + 1, :]
                put_turned(low_turned, low, chunk(part))

                @pl.when(part == 1)
                def _():
                    over_x(10, cross.at[side], cross.at[side]).start()

                down_copy(part).start()

            stage_core(
                lhs, rhs, units, first, ffn_c.at[block], second_copy(0, block, ffn_c, ffn_y)
            )
            return carry

        lax.fori_loop(0, 3, block_step, 0)

        def down_own(part, carry):
            hidden[chunk(part), :] += nn(
                hidden_units[2, at(own0 + part * BLOCK), :], w_down[...]
            )
            return carry

        lax.fori_loop(0, 2, down_own, 0)
        columns = 2 * width
        first = core_copy(3, 0, att_c, columns)
        stage_send(low_turned, mixed, columns, first)
        stage_core(low_turned, mixed, columns, first, att_c.at[0], second_copy(3, 0, att_c, att_y))

    pl.run_scoped(
        middle,
        pltpu.VMEM((half, features), BF16),
        pltpu.VMEM((rows, features), BF16),
        pltpu.VMEM((2, features, rows), BF16),
        pltpu.VMEM((features, units), BF16),
        pltpu.VMEM((features, units), BF16),
        pltpu.VMEM((units, features), BF16),
        pltpu.VMEM((3, rows, units), BF16),
        pltpu.VMEM((half, features), BF16),
        pltpu.VMEM((features, half), BF16),
        pltpu.VMEM((half, 2 * width), BF16),
    )

    def last(q_all, grads, k_all, v_all, slope_q, slope_k, heads_all, gate_all, pulls, weights, norm_out, norm_own, results, turned, tok_all):
        columns = 2 * width
        loads = [
            load(0, v, v_all.at[pl.ds(BAND, rows), :]),
            load(1, k, k_all.at[pl.ds(BAND, rows), :]),
            load(2, q, q_all.at[pl.ds(0, rows), :]),
            load(3, gate, gate_all),
            load(4, heads, heads_all),
            load(5, sq, slope_q),
            load(6, sk, slope_k),
        ]
        later = [load(7, tok, tok_all)] + [
            load(8 + i, source, weights.at[:, pl.ds(i * width, width)])
            for i, source in enumerate((wq, wk, wv, wg))
        ]
        for padded in (k_all, v_all):
            padded[:BAND, :] = jnp.zeros((BAND, width), BF16)
        for padded in (q_all, grads):
            padded[rows:, :] = jnp.zeros((BAND, width), BF16)
        gain_sum[0] = jnp.zeros(gain_sum.shape[1:], F32)
        for copy in loads:
            copy.wait()
        for part in range(2):
            mixed_copy(part).wait()
        over_x(10, cross.at[side], cross.at[side]).wait()

        def lane_rows(source, block):
            return to_column(
                jnp.concatenate(
                    [source(block * (BLOCK // 128) + i) for i in range(BLOCK // 128)], axis=0
                )
            )

        def prepare(block, carry):
            place = chunk(block)
            scale = lane_rows(lambda i: scale_rows[pl.ds(i, 1), :], block)
            per_half = half // 128
            joint = lane_rows(
                lambda i: cross[lax.div(i, per_half), pl.ds(lax.rem(i, per_half), 1), :], block
            )
            grad = mixed_grad[place, :].astype(F32)
            head_rows = heads_all[place, :].astype(F32)
            gain = gain_ref[0:1, :]
            scaled = grad * gate_all[place, :].astype(F32)
            unit = head_rows * scale
            gain_sum[0, 0:1, :] += jnp.sum(scaled * unit, axis=0, keepdims=True)
            pulls[1, place, width:] = (grad * (unit * gain)).astype(BF16)
            grads[place, :] = (
                scale * (scaled * gain)
                - head_rows * (scale * scale * scale) * (joint / full_inner)
            ).astype(BF16)
            return carry

        lax.fori_loop(0, rows // BLOCK, prepare, 0)
        gain_copy(0, 0, sibling).start()

        def seg_lanes(start, size):
            return seg_ref[0:1, pl.ds(pl.multiple_of(start, 128), size)]

        def seg_column(start):
            return to_column(
                jnp.concatenate([seg_lanes(start + i, 128) for i in range(0, BLOCK, 128)], axis=0)
            )

        def by_query(block, carry):
            place, span = chunk(block), pl.ds(pl.multiple_of(block * BLOCK, BLOCK), SPAN)
            row_at = iota_f32((BLOCK, 1), 0)
            key_at = iota_f32((1, SPAN), 1) - float(BAND)
            allowed = (seg_column(BAND + block * BLOCK) == seg_lanes(block * BLOCK, SPAN)) & (
                row_at >= key_at
            )
            for head in range(width // 128):
                lanes = slice(head * 128, head * 128 + 128)
                decay = decay_ref[head]
                falloff = jnp.exp(-decay * row_at) * jnp.exp(decay * key_at)
                grad = nt(grads[place, lanes], v_all[span, lanes])
                grad = jnp.where(allowed, grad * falloff, 0.0).astype(BF16)
                pulls[0, place, lanes] = (
                    nn(grad, k_all[span, lanes]) * slope_q[place, lanes].astype(F32)
                ).astype(BF16)
            return carry

        lax.fori_loop(0, rows // BLOCK, by_query, 0)

        def by_key(block, carry):
            place, span = chunk(block), pl.ds(pl.multiple_of(block * BLOCK, BLOCK), SPAN)
            here = pl.ds(pl.multiple_of(BAND + block * BLOCK, 128), BLOCK)
            key_at = iota_f32((BLOCK, 1), 0)
            row_at = iota_f32((1, SPAN), 1)
            allowed = (
                seg_column(BAND + block * BLOCK) == seg_lanes(BAND + block * BLOCK, SPAN)
            ) & (row_at >= key_at)
            for head in range(width // 128):
                lanes = slice(head * 128, head * 128 + 128)
                turned_lanes = slice(width + head * 128, width + head * 128 + 128)
                decay = decay_ref[head]
                falloff = jnp.exp(decay * key_at) * jnp.exp(-decay * row_at)
                span_q, span_grad = q_all[span, lanes], grads[span, lanes]
                scores = nt(k_all[here, lanes], span_q)
                weighted = jnp.where(allowed, scores * falloff, 0.0).astype(BF16)
                pulls[1, place, lanes] = nn(weighted, span_grad).astype(BF16)
                grad = nt(v_all[here, lanes], span_grad)
                grad = jnp.where(allowed, grad * falloff, 0.0).astype(BF16)
                pulls[0, place, turned_lanes] = (
                    nn(grad, span_q) * slope_k[place, lanes].astype(F32)
                ).astype(BF16)
            return carry

        lax.fori_loop(0, rows // BLOCK, by_key, 0)
        for copy in later:
            copy.wait()

        def normed_part(step, carry):
            part = lax.rem(step, 2)
            place = at((1 - side + lax.div(step, 2) * (2 * side - 1)) * half + part * BLOCK)
            back = nt(pulls[0, place, :], weights[:, :columns]) + nt(
                pulls[1, place, :], weights[:, columns:]
            )

            @pl.when(step < 2)
            def _():
                norm_out[chunk(part), :] = back.astype(BF16)
                norm_copy(norm_out, part).start()

            @pl.when(step >= 2)
            def _():
                norm_own[chunk(part), :] = back

            return carry

        lax.fori_loop(0, 4, normed_part, 0)

        def turn(block, carry):
            source = tok_all[chunk(block), :].astype(F32)
            put_turned(turned, (source * rms_scale(source)).astype(BF16), chunk(block))
            return carry

        lax.fori_loop(0, rows // BLOCK, turn, 0)

        gain_copy(0, 0, sibling).wait()
        gain_sum[1] = gain_sum[0] + gain_in[0]
        gain_copy(1, 1, beside).start()

        def block_step(step, carry):
            block = step + 1
            rhs = pulls.at[step]
            first = core_copy(3, block, att_c, columns)
            stage_send(turned, rhs, columns, first)
            stage_core(
                turned, rhs, columns, first, att_c.at[block], second_copy(3, block, att_c, att_y)
            )
            return carry

        lax.fori_loop(0, 2, block_step, 0)

        def seconds(block, carry):
            stage_second(0, block, ffn_c, ffn_y, ffn_z)
            return carry

        lax.fori_loop(0, 3, seconds, 0)

        def finish_out(part, carry):
            down_copy(part).wait()
            results[0, chunk(part), :] = (
                hidden[chunk(part), :] + down_in[chunk(part), :].astype(F32)
            ).astype(BF16)
            out_copy(results.at[0], part).start()
            pltpu.make_async_copy(
                results.at[0, chunk(part), :], out_ref.at[at(own0 + part * BLOCK), :], local.at[part]
            ).start()
            return carry

        lax.fori_loop(0, 2, finish_out, 0)
        gain_copy(1, 1, beside).wait()
        gain_sum[2] = gain_sum[1] + gain_in[1]
        for hop in range(1, thirds):
            gain_copy(2, 1 + hop, far(hop)).start()

        def finish_tokens(part, carry):
            norm_copy(norm_out, part).wait()
            pulled = norm_own[chunk(part), :] + norm_in[chunk(part), :].astype(F32)
            source = tok_all[at(own0 + part * BLOCK), :].astype(F32)
            results[1, chunk(part), :] = (
                grad_hidden[chunk(part), :] + rms_back(source, rms_scale(source), pulled)
            ).astype(BF16)
            tg_copy(results.at[1], part).start()
            pltpu.make_async_copy(
                results.at[1, chunk(part), :], tg_ref.at[at(own0 + part * BLOCK), :], local.at[2 + part]
            ).start()
            return carry

        lax.fori_loop(0, 2, finish_tokens, 0)

        def seconds_last(block, carry):
            stage_second(3, block, att_c, att_y, att_z)
            return carry

        lax.fori_loop(0, 3, seconds_last, 0)

        def ffn_total(block, carry):
            ffn_ref[block] = stage_third(0, block, ffn_y, ffn_z)
            return carry

        lax.fori_loop(0, 3, ffn_total, 0)

        def attn_total(block, carry):
            attn_ref[block] = stage_third(3, block, att_y, att_z)
            return carry

        lax.fori_loop(0, 1, attn_total, 0)
        turn_out[...] = attn_ref[0, :, width:]
        turn_copy = over_x(19, turn_out, turn_in)
        turn_copy.start()
        lax.fori_loop(1, 3, attn_total, 0)
        total = gain_sum[2]
        for hop in range(1, thirds):
            gain_copy(2, 1 + hop, far(hop)).wait()
            total = total + gain_in[1 + hop]
        gain_out[...] = total
        turn_copy.wait()
        attn_ref[0, :, :width] += turn_in[...]

        def close(part, carry):
            out_copy(results.at[0], part).wait()
            tg_copy(results.at[1], part).wait()
            for index, target in ((0, out_ref), (1, tg_ref)):
                pltpu.make_async_copy(
                    results.at[index, chunk(part), :],
                    target.at[at(own0 + part * BLOCK), :],
                    local.at[2 * index + part],
                ).wait()
            return carry

        lax.fori_loop(0, 2, close, 0)

    pl.run_scoped(
        last,
        pltpu.VMEM((rows + BAND, width), BF16),
        pltpu.VMEM((rows + BAND, width), BF16),
        pltpu.VMEM((rows + BAND, width), BF16),
        pltpu.VMEM((rows + BAND, width), BF16),
        pltpu.VMEM((rows, width), BF16),
        pltpu.VMEM((rows, width), BF16),
        pltpu.VMEM((rows, width), BF16),
        pltpu.VMEM((rows, width), BF16),
        pltpu.VMEM((2, rows, 2 * width), BF16),
        pltpu.VMEM((features, 4 * width), BF16),
        pltpu.VMEM((half, features), BF16),
        pltpu.VMEM((half, features), F32),
        pltpu.VMEM((2, half, features), BF16),
        pltpu.VMEM((features, rows), BF16),
        pltpu.VMEM((rows, features), BF16),
    )


def run_rest(ways, *args):
    (seg, decays, sums, gain, tok, cot, u, wo, wo_part, wl) = args[:10]
    rows, features = tok.shape
    width, units = u.shape[1], wl.shape[1]
    half, thirds, share = rows // 2, ways // 4, features // ways
    quarter = features // 4
    vmem = pl.BlockSpec(memory_space=pltpu.VMEM)
    hbm = pl.BlockSpec(memory_space=pl.ANY)
    shape = jax.ShapeDtypeStruct
    scratch = [
        ((rows, features), BF16), ((half, width), BF16), ((width, features), BF16),
        (sums.shape, F32), ((half, features), BF16), ((half, features), BF16),
        ((rows, width), BF16), ((2, 8, 128), F32), ((half, features), BF16), ((share, width), F32),
        ((3, 2 * quarter, units), BF16), ((3, quarter, units), BF16),
        ((3, thirds - 1, share, units), BF16),
        ((3, 2 * quarter, 2 * width), BF16), ((3, quarter, 2 * width), BF16),
        ((3, thirds - 1, share, 2 * width), BF16), ((thirds + 1, 8, width), F32),
        ((half, width), BF16), ((width, features), BF16), ((half, width), BF16),
        ((half, features), BF16), ((half, features), F32), ((half, features), F32),
        (sums.shape, F32), ((2 * quarter, max(units, 2 * width)), BF16), ((3, 8, width), F32),
        ((share, width), F32),
    ]
    return pl.pallas_call(
        functools.partial(rest, ways),
        in_specs=[vmem, pl.BlockSpec(memory_space=pltpu.SMEM), vmem, vmem] + [hbm] * (len(args) - 4),
        out_specs=[hbm, hbm, vmem, vmem, vmem],
        out_shape=[
            shape((rows, features), BF16), shape((rows, features), BF16),
            shape((3, share, units), F32), shape((3, share, 2 * width), F32), shape((8, width), F32),
        ],
        scratch_shapes=[pltpu.VMEM(size, dtype) for size, dtype in scratch]
        + [
            pltpu.SemaphoreType.DMA((20,)), pltpu.SemaphoreType.DMA((20,)),
            pltpu.SemaphoreType.DMA((2, 6)), pltpu.SemaphoreType.DMA((2, 6)),
            pltpu.SemaphoreType.DMA((7, thirds + 1)), pltpu.SemaphoreType.DMA((7, thirds + 1)),
            pltpu.SemaphoreType.DMA((12,)),
        ],
        compiler_params=pltpu.CompilerParams(
            collective_id=1, has_side_effects=True, vmem_limit_bytes=VMEM_LIMIT
        ),
        cost_estimate=pl.CostEstimate(flops=5 * 10**10, bytes_accessed=60 * 2**20, transcendentals=10**6),
        name="rest",
    )(*args)


def local(
    ways, tokens, segment_ids, decay_rate, query_weight, key_weight, value_weight, gate_weight,
    output_weight, norm_gain, left_weight, right_weight, down_weight, cotangent,
):
    heads_here, head_size = norm_gain.shape
    width = heads_here * head_size
    gain = norm_gain.astype(F32).reshape(1, width)
    segments = jnp.pad(
        segment_ids.astype(F32).reshape(1, -1), ((0, 0), (BAND, BAND)), constant_values=-1.0
    )
    core = lax.rem(lax.axis_index("dp"), 2)
    part = lax.dynamic_slice_in_dim(output_weight, core * (width // 2), width // 2, 0)
    part = lax.ppermute(part, "tensor", [(0, 1), (1, 0)])
    u, heads, gate, q, k, v, sq, sk, sums = run_attend(
        segments, decay_rate, tokens, query_weight, key_weight, value_weight, gate_weight, gain
    )
    block_out, tokens_grad, ffn, attn, gain_total = run_rest(
        ways, segments, decay_rate, sums, gain, tokens, cotangent, u, output_weight, part,
        left_weight, right_weight, down_weight, query_weight, key_weight, value_weight, gate_weight,
        heads, gate, q, k, v, sq, sk,
    )
    each = head_size // ways
    gain_grad = lax.dynamic_slice_in_dim(
        gain_total[0].reshape(heads_here, head_size), lax.axis_index("dp") * each, each, 1
    )
    return (
        block_out,
        tokens_grad.astype(F32),
        attn[1, :, :width],
        attn[1, :, width:],
        attn[2, :, :width],
        attn[2, :, width:],
        attn[0, :, :width].T,
        gain_grad,
        ffn[0],
        ffn[1],
        ffn[2].T,
    )


def solution(mesh):
    dp, tensor = "dp", "tensor"
    in_specs = (
        P(dp, None), P(dp, None), P(tensor), P(None, tensor), P(None, tensor), P(None, tensor),
        P(None, tensor), P(tensor, None), P(tensor, None), P(None, tensor), P(None, tensor),
        P(tensor, None), P(dp, None),
    )
    out_specs = (
        P(dp, None), P(dp, None), P(dp, tensor), P(dp, tensor), P(dp, tensor), P(dp, tensor),
        P(tensor, dp), P(tensor, dp), P(dp, tensor), P(dp, tensor), P(tensor, dp),
    )
    return jax.shard_map(
        functools.partial(local, mesh.shape[dp]),
        mesh=mesh, in_specs=in_specs, out_specs=out_specs, check_vma=False,
    )
```

time: 1140 us -> 236 us (0.21)
  waiting for transfers between devices: 898 us -> 0.01 us
  Pallas kernels: 0 us -> 218 us
  matrix products: 126 us -> 0 us
  blocking collectives: 42.7 us -> 0 us
  other arithmetic: 32.2 us -> 4.43 us
  between operations: 15.6 us -> 0.7 us
    reduce_scatter x8 -> x0, waiting for transfers between devices: 572 us -> none  [the longest x1 85.7 us: local(): lax.psum_scatter(down_grad, 'dp', scatter_dimension=1, tiled=True)]
    psum x3 -> x0, waiting for transfers between devices: 326 us -> none  [tensor_sum(): return lax.psum(values, 'tensor')]
    pallas_call x0 -> x2, Pallas kernels: none -> 218 us  [the longest x1 204 us: run_rest(): pl.pallas_call(functools.partial(rest, ways), in_specs=[vmem, pl.BlockSpe...]
    dot_general x36 -> x0, matrix products: 126 us -> none  [the longest x8 47.6 us: product_tn(): lax.dot_general(left_op, right_op, (((0,), (0,)), ((), ())), preferred_el...]
    unnamed x1 -> x0, blocking collectives: 31.7 us -> none
    unnamed x118 -> x7, local copies, waits for them, and re-layouts: 19.2 us -> 2.13 us
    reduce_sum x5 -> x0, other arithmetic: 13.3 us -> none  [the longest x2 7.62 us: rms_back(): jnp.mean(values * grads, axis=1, keepdims=True)]
  transfers between devices with their start and end apart: 11 -> 1, of which waited for: 11 -> 0; matrix products, arithmetic and copies ran while one was open for 6% -> 1% of each run, Pallas kernels for 0% -> 6%
where the time goes in v2:
time: 236 us; the launch traced here: 235 us
  Pallas kernels  218 us (92%)
  local copies, waits for them, and re-layouts  9.52 us (4%)
  other arithmetic  4.43 us (2%)
  starting transfers between devices  3 us (1%)
    pallas_call x1, Pallas kernels, run_rest(): pl.pallas_call(functools.partial(rest, ways), in_specs=[vmem, pl.BlockSpe...  204 us
    pallas_call x1, Pallas kernels, run_attend(): pl.pallas_call(attend, grid=(rows // BLOCK,), in_specs=[whole(*segments.s...  13.9 us
  transfers between devices with their start and end apart: 1, of which 0 were waited for; matrix products, arithmetic and copies ran while one was open for 1% of the time, Pallas kernels for 6%

profile of v2, /device:TPU:0, one launch (start us, length us, event | category | flops | bytes accessed | tf_op | source)
XLA Modules:
  0.0 235.2 jit_solution(9731279756140324734)
XLA Ops:
  0.7 1.1 constant_dynamic-slice_fusion.1
  1.7 3.0 %collective-permute-start = (bf16[256,1024]{1,0:T(8,128)(2,1)S(1)}, bf16[256,1024]{1,0:T(8,128)(2,1)S(1)}, u32[]{:S(2)}, u32[]{:S(2)}) collective-permute-start(bf16[256,1024]{1,0:T(8,128)(2,1)S(1)} %constant_dynamic-slice_fusion.1), channel_id=1, source_target_pairs={{0,1},{1,0},{2,3},{3,2},{4,5},{5,4},{6,7},{7,6},{8,9},{9,8},{10,11... | collective-permute-start | bytes 1572872 | tf_op jit(solution)/shard_map/ppermute | solution.py:808
  4.7 1.3 reshape.29
  6.0 0.7 convert_element_type.7
  6.7 0.6 pad.4.seg_ref
  7.3 13.9 %attend.1 = (bf16[1024,512]{1,0:T(8,128)(2,1)}, bf16[1024,512]{1,0:T(8,128)(2,1)}, bf16[1024,512]{1,0:T(8,128)(2,1)}, bf16[1024,512]{1,0:T(8,128)(2,1)}, bf16[10...) custom-call(f32[1,1792]{1,0:T(1,128)} %pad.4.seg_ref, ...), custom_call_target="tpu_custom_call" | custom-call | flops 6000000000 | bytes 15728640 | tf_op jit(solution)/shard_map/attend/pallas_call | solution.py:138
  21.2 0.0 collective-permute-done.wo_part
  21.3 0.0 copy-start.2
  21.3 0.8 copy-done.2
  22.1 203.6 %rest.1 = (bf16[1024,1024]{1,0:T(8,128)(2,1)}, bf16[1024,1024]{1,0:T(8,128)(2,1)}, f32[3,64,1408]{2,1,0:T(8,128)}, f32[3,64,1024]{2,1,0:T(8,128)}, f32[8,512]{1,0:T(8,128)}) custom-call(f32[1,1792]{1,0:T(1,128)} %pad.4.seg_ref, f32[4]{0:T(128)} %decay_ref.3, f32[8,128]{1,0:T(8,128)} %get-tuple-element.25.sums_ref, f32[1,512]{1,0:T(1,128)} %bitcast.24, ...), custom_call_target="tpu_custom_call" | custom-call | flops 49999998976 | bytes 62914560 | tf_op jit(solution)/shard_map/rest/pallas_call | solution.py:773
  225.7 0.0 copy-start
  225.7 0.9 slice.32
  226.5 2.0 slice_bitcast_fusion.3
  228.5 2.2 slice_bitcast_fusion
  230.7 0.0 copy-done
  230.7 0.0 copy-start.1
  230.7 2.5 %convert_element_type.8 = f32[1024,1024]{1,0:T(8,128)} convert(bf16[1024,1024]{1,0:T(8,128)(2,1)S(1)} %copy-done) | non-fusion elementwise | flops 1048576 | bytes 6291456 | tf_op jit(solution)/shard_map/convert_element_type | solution.py:823
  233.2 0.6 constant_dynamic-slice_fusion
  233.9 0.0 copy-done.1
  233.9 1.3 copy.25
Async XLA Ops:
  1.7 19.5 %collective-permute-start = (bf16[256,1024]{1,0:T(8,128)(2,1)S(1)}, bf16[256,1024]{1,0:T(8,128)(2,1)S(1)}, u32[]{:S(2)}, u32[]{:S(2)}) collective-permute-start(bf16[256,1024]{1,0:T(8,128)(2,1)S(1)} %constant_dynamic-slice_fusion.1), channel_id=1, source_target_pairs={{0,1},{1,0},{2,3},{3,2},{4,5},{5,4},{6,7},{7,6},{8,9},{9,8},{10,11... | collective-permute-start | bytes 1572872 | tf_op jit(solution)/shard_map/ppermute | solution.py:808
  21.3 0.8 copy-start.2
  225.7 5.1 %copy-start = (bf16[1024,1024]{1,0:T(8,128)(2,1)S(1)}, bf16[1024,1024]{1,0:T(8,128)(2,1)}, u32[]{:S(2)}) copy-start(bf16[1024,1024]{1,0:T(8,128)(2,1)} %get-tuple-element.35) | copy-start | bytes 6291460
  230.7 3.1 %copy-start.1 = (bf16[1024,1024]{1,0:T(8,128)(2,1)S(1)}, bf16[1024,1024]{1,0:T(8,128)(2,1)}, u32[]{:S(2)}) copy-start(bf16[1024,1024]{1,0:T(8,128)(2,1)} %get-tuple-element.58) | copy-start | bytes 6291460

commit v3 on v2

--- a/solution.py
+++ b/solution.py
@@ -66,108 +66,19 @@
     return lax.broadcasted_iota(jnp.int32, shape, axis).astype(F32)
 
 
-def attend(
-    seg_ref, decay_ref, tok_ref, wq_ref, wk_ref, wv_ref, wg_ref, gain_ref,
-    u_ref, heads_ref, gate_ref, q_ref, k_ref, v_ref, sq_ref, sk_ref, sums_ref,
-    k_all, v_all,
-):
-    step = pl.program_id(0)
-    width = q_ref.shape[1]
-
-    @pl.when(step == 0)
-    def _():
-        k_all[:BAND, :] = jnp.zeros((BAND, width), BF16)
-        v_all[:BAND, :] = jnp.zeros((BAND, width), BF16)
-
-    source = tok_ref[...].astype(F32)
-    normed = (source * rms_scale(source)).astype(BF16)
-    pre = nn(normed, wk_ref[...])
-    sigma = jax.nn.sigmoid(pre)
-    key_rows = (pre * sigma).astype(BF16)
-    sk_ref[...] = (sigma * (1.0 + pre * (1.0 - sigma))).astype(BF16)
-    k_ref[...] = key_rows
-    here = pl.ds(pl.multiple_of(BAND + step * BLOCK, 128), BLOCK)
-    k_all[here, :] = key_rows
-    value_rows = nn(normed, wv_ref[...]).astype(BF16)
-    v_ref[...] = value_rows
-    v_all[here, :] = value_rows
-    pre = nn(normed, wq_ref[...])
-    sigma = jax.nn.sigmoid(pre)
-    queries = (pre * sigma).astype(BF16)
-    sq_ref[...] = (sigma * (1.0 + pre * (1.0 - sigma))).astype(BF16)
-    q_ref[...] = queries
-    gate = nn(normed, wg_ref[...])
-    gate_ref[...] = gate.astype(BF16)
-
-    span = pl.ds(pl.multiple_of(step * BLOCK, BLOCK), SPAN)
-    seg_keys = seg_ref[0:1, span]
-    seg_rows = to_column(
-        jnp.concatenate(
-            [
-                seg_ref[0:1, pl.ds(pl.multiple_of(BAND + step * BLOCK + i, 128), 128)]
-                for i in range(0, BLOCK, 128)
-            ],
-            axis=0,
-        )
-    )
-    row_at = iota_f32((BLOCK, 1), 0)
-    key_at = iota_f32((1, SPAN), 1) - float(BAND)
-    allowed = (seg_rows == seg_keys) & (row_at >= key_at)
-    total = jnp.zeros((BLOCK, 1), F32)
-    for head in range(width // 128):
-        lanes = slice(head * 128, head * 128 + 128)
-        decay = decay_ref[head]
-        scores = nt(queries[:, lanes], k_all[span, lanes])
-        falloff = jnp.exp(-decay * row_at) * jnp.exp(decay * key_at)
-        weighted = jnp.where(allowed, scores * falloff, 0.0).astype(BF16)
-        heads = nn(weighted, v_all[span, lanes])
-        total = total + jnp.sum(heads * heads, axis=1, keepdims=True)
-        heads_ref[:, lanes] = heads.astype(BF16)
-        u_ref[:, lanes] = (heads * gain_ref[0:1, lanes] * gate[:, lanes]).astype(BF16)
-    for part in range(BLOCK // 128):
-        sums_ref[pl.ds(step * (BLOCK // 128) + part, 1), :] = to_rows(
-            total[part * 128 : part * 128 + 128, :]
-        )
-
-
-def run_attend(segments, decays, tokens, wq, wk, wv, wg, gain):
-    rows, features = tokens.shape
-    width = wq.shape[1]
-    whole = lambda *shape: pl.BlockSpec(shape, lambda i: (0,) * len(shape))
-    block = lambda columns: pl.BlockSpec((BLOCK, columns), lambda i: (i, 0))
-    return pl.pallas_call(
-        attend,
-        grid=(rows // BLOCK,),
-        in_specs=[
-            whole(*segments.shape),
-            pl.BlockSpec(memory_space=pltpu.SMEM),
-            block(features),
-            whole(features, width), whole(features, width), whole(features, width), whole(features, width),
-            whole(1, width),
-        ],
-        out_specs=[block(width)] * 8 + [whole(rows // 128, 128)],
-        out_shape=[jax.ShapeDtypeStruct((rows, width), BF16)] * 8
-        + [jax.ShapeDtypeStruct((rows // 128, 128), F32)],
-        scratch_shapes=[pltpu.VMEM((BAND + rows, width), BF16)] * 2,
-        compiler_params=pltpu.CompilerParams(vmem_limit_bytes=VMEM_LIMIT),
-        cost_estimate=pl.CostEstimate(flops=6 * 10**9, bytes_accessed=15 * 2**20, transcendentals=10**6),
-        name="attend",
-    )(segments, decays, tokens, wq, wk, wv, wg, gain)
-
-
 def tiles(extent, most=512):
     return [(start, min(most, extent - start)) for start in range(0, extent, most)]
 
 
-def rest(
+def layer(
     ways,
-    seg_ref, decay_ref, sums_ref, gain_ref, tok, cot, u, wo, wo_part, wl, wr, wd, wq, wk, wv, wg,
-    heads, gate, q, k, v, sq, sk,
+    ids_ref, decay_ref, gain_ref, tok, cot, wo, wl, wr, wd, wq, wk, wv, wg,
     out_ref, tg_ref, ffn_ref, attn_ref, gain_out,
-    lifted, u_in, wo_peer, sum_in, back_in, down_in, mixed_grad, cross, norm_in, turn_in,
+    q, k, v, gate, heads, sq, sk,
+    u_in, wo_peer, sum_in, back_in, down_in, mixed_grad, cross, norm_in, turn_in,
     ffn_c, ffn_y, ffn_z, att_c, att_y, att_z, gain_in,
-    u_own, wo_own, mixed_out, down_out, hidden, grad_hidden, scale_rows, core_out, gain_sum, turn_out,
-    send, recv, dp_send, dp_recv, z_send, z_recv, local,
+    seg_ref, sums_ref, u_all, wo_own, mixed_out, down_out, hidden, grad_hidden, scale_rows, core_out, gain_sum, turn_out,
+    send, recv, dp_send, dp_recv, z_send, z_recv, local, kept,
 ):
     dp, side = lax.axis_index("dp"), lax.axis_index("tensor")
     core, second, third = lax.rem(dp, 2), lax.rem(lax.div(dp, 2), 2), lax.div(dp, 4)
@@ -211,32 +122,50 @@
     def chunk(part):
         return at(part * BLOCK)
 
-    def u_copy(part):
-        return over_x(part, u.at[at(other0 + part * BLOCK), :], u_in.at[chunk(part), :])
-
-    def lifted_copy(part):
-        place = lifted.at[at(own0 + part * BLOCK), :]
-        return over_x(4 + part, place, place)
+    def u_copy(block):
+        return over_x(block, u_all.at[chunk(block), :], u_in.at[chunk(block), :])
+
+    def sum_copy(block):
+        return over_x(4 + block, sums_ref.at[block], sum_in.at[block])
 
     def back_copy(source, part):
-        return over_x(6 + part, source.at[chunk(part), :], back_in.at[chunk(part), :])
+        return over_x(11 + part, source.at[chunk(part), :], back_in.at[chunk(part), :])
 
     def mixed_copy(part):
         return over_x(
-            8 + part, mixed_out.at[chunk(part), :], mixed_grad.at[at(own0 + part * BLOCK), :]
+            13 + part, mixed_out.at[chunk(part), :], mixed_grad.at[at(own0 + part * BLOCK), :]
         )
 
+    def cross_copy(part):
+        mine = cross.at[side * 2 + part]
+        return over_x(15 + part, mine, mine)
+
     def down_copy(part):
-        return over_x(11 + part, down_out.at[chunk(part), :], down_in.at[chunk(part), :])
+        return over_x(17 + part, down_out.at[chunk(part), :], down_in.at[chunk(part), :])
 
     def norm_copy(source, part):
-        return over_x(13 + part, source.at[chunk(part), :], norm_in.at[chunk(part), :])
+        return over_x(19 + part, source.at[chunk(part), :], norm_in.at[chunk(part), :])
 
     def out_copy(source, part):
-        return over_x(15 + part, source.at[chunk(part), :], out_ref.at[at(own0 + part * BLOCK), :])
+        return over_x(21 + part, source.at[chunk(part), :], out_ref.at[at(own0 + part * BLOCK), :])
 
     def tg_copy(source, part):
-        return over_x(17 + part, source.at[chunk(part), :], tg_ref.at[at(own0 + part * BLOCK), :])
+        return over_x(23 + part, source.at[chunk(part), :], tg_ref.at[at(own0 + part * BLOCK), :])
+
+    slice_rows = width // 4
+    wo_start = core * (2 * slice_rows) + second * slice_rows
+    wo_piece = pl.ds(pl.multiple_of(wo_start, slice_rows), slice_rows)
+
+    def wo_across():
+        return over_x(8, wo.at[wo_piece, :], wo_peer.at[wo_piece, :])
+
+    def wo_beside():
+        piece = wo_peer.at[wo_piece, :]
+        return remote(piece, piece, send.at[9], recv.at[9], beside)
+
+    def wo_sibling():
+        piece = wo_peer.at[pl.ds(pl.multiple_of(core * (2 * slice_rows), 2 * slice_rows), 2 * slice_rows), :]
+        return remote(piece, piece, send.at[10], recv.at[10], sibling)
 
     def core_copy(first, block, landing, columns):
         return remote(
@@ -313,85 +242,137 @@
     partners = [across, sibling, beside] + [far(hop) for hop in range(1, thirds)]
     for device in partners:
         pl.semaphore_signal(barrier, inc=1, device_id=device, device_id_type=MESH)
-    pl.semaphore_wait(barrier, len(partners))
-
-    def middle(tok_own, cot_all, turned, w_left, w_right, w_down, hidden_units, back_out, low_turned, mixed):
-        part_copy = load(1, wo_part, wo_peer.at[at(core * BLOCK), :])
-        loads = [
-            load(0, wo, wo_own),
-            load(2, u.at[pl.ds(pl.multiple_of(own0, BLOCK), half), :], u_own),
-            load(3, tok.at[pl.ds(pl.multiple_of(own0, BLOCK), half), :], tok_own),
-            load(4, cot, cot_all),
-        ]
-        weights = [load(5, wl, w_left), load(6, wr, w_right), load(7, wd, w_down)]
-        for part in range(2):
-            u_copy(part).start()
-        sum_copy = over_x(2, sums_ref, sum_in)
-        sum_copy.start()
-        part_copy.wait()
-        quarter = wo_peer.at[at(core * BLOCK), :]
-        quarter_copy = remote(quarter, quarter, send.at[3], recv.at[3], sibling)
-        quarter_copy.start()
-        for copy in loads:
+
+    def seg_lanes(start, size):
+        return seg_ref[0:1, pl.ds(pl.multiple_of(start, 128), size)]
+
+    def seg_column(start):
+        return to_column(
+            jnp.concatenate([seg_lanes(start + i, 128) for i in range(0, BLOCK, 128)], axis=0)
+        )
+
+    def gain_lanes(head):
+        return gain_ref[head : head + 1, :].astype(F32)
+
+    blocks = rows // BLOCK
+    lanes_in = BLOCK // 128
+
+    def lane_column(source, block):
+        return to_column(
+            jnp.concatenate([source[block, i : i + 1, :] for i in range(lanes_in)], axis=0)
+        )
+
+    def middle(lifted, cot_all, turned, w_left, w_right, w_down, hidden_units, back_out, low_turned):
+        tok_all = hidden_units.at[2, :, pl.ds(0, features)]
+        halves = (pl.ds(0, width), pl.ds(width, width))
+        w_query, w_key = (hidden_units.at[0, :, cut] for cut in halves)
+        w_value, w_gate = (hidden_units.at[1, :, cut] for cut in halves)
+        q_all, gate_all = (turned.at[0, :, cut] for cut in halves)
+        slope_q, slope_k = (turned.at[1, :, cut] for cut in halves)
+        heads_all = low_turned
+        k_all, v_all = (w_down.at[:, cut] for cut in halves)
+        k_rows, v_rows = (whole.at[pl.ds(BAND, rows), :] for whole in (k_all, v_all))
+
+        first = [load(0, tok, tok_all), load(1, wk, w_key), load(2, wv, w_value), load(3, wq, w_query), load(4, wg, w_gate)]
+        pl.semaphore_wait(barrier, len(partners))
+        wo_across().start()
+        pad = jnp.full((1, BAND), -1.0, F32)
+        seg_ref[0:1, :BAND] = pad
+        seg_ref[0:1, BAND + rows :] = pad
+        seg_ref[0:1, BAND : BAND + rows] = ids_ref[...].astype(F32)
+        for padded in (k_all, v_all):
+            padded[:BAND, :] = jnp.zeros((BAND, width), BF16)
+        for copy in first:
             copy.wait()
-
-        def own_heads(part, carry):
-            grad_hidden[chunk(part), :] = nn(u_own[chunk(part), :], wo_own[...])
-            return carry
-
-        lax.fori_loop(0, 2, own_heads, 0)
-
-        def turn(part, carry):
-            put_turned(turned.at[1], cot_all[chunk(part), :], chunk(part))
-            return carry
-
-        lax.fori_loop(0, rows // BLOCK, turn, 0)
-        quarter_copy.wait()
-        sum_copy.wait()
-        scale_rows[...] = lax.rsqrt((sums_ref[...] + sum_in[...]) / full_inner + eps)
-
-        def scale_of(block):
-            return to_column(
-                jnp.concatenate(
-                    [
-                        scale_rows[pl.ds(block * (BLOCK // 128) + i, 1), :]
-                        for i in range(BLOCK // 128)
-                    ],
-                    axis=0,
+        later = [load(5, wo, wo_own), load(6, cot, cot_all), load(7, wl, w_left), load(8, wr, w_right)]
+        keeps = [(q_all, q), (k_rows, k), (v_rows, v), (gate_all, gate), (slope_q, sq), (slope_k, sk), (heads_all, heads)]
+
+        def forward_block(block, carry):
+            place = chunk(block)
+            here = pl.ds(pl.multiple_of(BAND + block * BLOCK, 128), BLOCK)
+            span = pl.ds(pl.multiple_of(block * BLOCK, BLOCK), SPAN)
+            source = tok_all[place, :].astype(F32)
+            normed = (source * rms_scale(source)).astype(BF16)
+            for weight, slope, target, rows_at in ((w_key, slope_k, k_all, here), (w_query, slope_q, q_all, place)):
+                pre = nn(normed, weight[...])
+                sigma = jax.nn.sigmoid(pre)
+                target[rows_at, :] = (pre * sigma).astype(BF16)
+                slope[place, :] = (sigma * (1.0 + pre * (1.0 - sigma))).astype(BF16)
+            v_all[here, :] = nn(normed, w_value[...]).astype(BF16)
+            gate_all[place, :] = nn(normed, w_gate[...]).astype(BF16)
+            row_at = iota_f32((BLOCK, 1), 0)
+            key_at = iota_f32((1, SPAN), 1) - float(BAND)
+            allowed = (seg_column(BAND + block * BLOCK) == seg_lanes(block * BLOCK, SPAN)) & (
+                row_at >= key_at
+            )
+            total = jnp.zeros((BLOCK, 1), F32)
+            for head in range(width // 128):
+                lanes = slice(head * 128, head * 128 + 128)
+                decay = decay_ref[head]
+                falloff = jnp.exp(-decay * row_at) * jnp.exp(decay * key_at)
+                scores = nt(q_all[place, lanes], k_all[span, lanes])
+                weighted = jnp.where(allowed, scores * falloff, 0.0).astype(BF16)
+                found = nn(weighted, v_all[span, lanes])
+                total = total + jnp.sum(found * found, axis=1, keepdims=True)
+                heads_all[place, lanes] = found.astype(BF16)
+                u_all[place, lanes] = (
+                    found * gain_lanes(head) * gate_all[place, lanes].astype(F32)
+                ).astype(BF16)
+            lane_rows = to_rows(total)
+            for i in range(lanes_in):
+                sums_ref[block, i : i + 1, :] = lane_rows[i : i + 1, :]
+            u_copy(block).start()
+            sum_copy(block).start()
+            for index, (source, target) in enumerate(keeps):
+                pltpu.make_async_copy(
+                    source.at[place, :], target.at[place, :], kept.at[index]
+                ).start()
+
+            @pl.when(block == 1)
+            def _():
+                wo_across().wait()
+                wo_beside().start()
+
+            @pl.when(block == blocks - 1)
+            def _():
+                wo_beside().wait()
+                wo_sibling().start()
+
+            return carry
+
+        lax.fori_loop(0, blocks, forward_block, 0)
+        for index, (source, target) in enumerate(keeps):
+            pltpu.make_async_copy(source, target, kept.at[index]).wait()
+        later.append(load(9, wd, w_down))
+        for copy in later:
+            copy.wait()
+        wo_sibling().wait()
+
+        def gated(step, carry):
+            block = lax.rem(step + 1 - side, blocks)
+            part = lax.rem(block, 2)
+            owned = lax.div(block, 2) == side
+            place = chunk(block)
+            u_copy(block).wait()
+            sum_copy(block).wait()
+            for i in range(lanes_in):
+                scale_rows[block, i : i + 1, :] = lax.rsqrt(
+                    (sums_ref[block, i : i + 1, :] + sum_in[block, i : i + 1, :]) / full_inner + eps
                 )
-            )
-
-        def open_chunk(part, carry):
-            u_copy(part).wait()
-            scale = scale_of(side * (half // BLOCK) + part)
-            from_peer = u_in[chunk(part), :]
-            attn = grad_hidden[chunk(part), :] + nn(from_peer, wo_peer[...])
-            state = tok_own[chunk(part), :].astype(F32) + scale * attn
-            hidden[chunk(part), :] = state
-            lifted[at(own0 + part * BLOCK), :] = (state * rms_scale(state)).astype(BF16)
-            lifted_copy(part).start()
-            mixed[chunk(part), :width] = (u_own[chunk(part), :].astype(F32) * scale).astype(BF16)
-            mixed[chunk(part), width:] = (from_peer.astype(F32) * scale).astype(BF16)
-            return carry
-
-        lax.fori_loop(0, 2, open_chunk, 0)
-        for copy in weights:
-            copy.wait()
-
-        def gated(step, carry):
-            part = lax.rem(step, 2)
-            place = at((side + lax.div(step, 2) * (1 - 2 * side)) * half + part * BLOCK)
-
-            @pl.when(step >= 2)
+            attn = nn(u_all[place, :], wo_own[...]) + nn(u_in[place, :], wo_peer[...])
+            state = tok_all[place, :].astype(F32) + lane_column(scale_rows, block) * attn
+            rows_in = (state * rms_scale(state)).astype(BF16)
+            lifted[...] = rows_in
+
+            @pl.when(owned)
             def _():
-                lifted_copy(part).wait()
-
-            rows_in = lifted[place, :]
+                hidden[chunk(part), :] = state
+
             rows_cot = cot_all[place, :]
             for start, size in tiles(units):
                 cut = slice(start, start + size)
-                left = nn(rows_in, w_left[:, cut])
-                right = nn(rows_in, w_right[:, cut])
+                left = nn(lifted[...], w_left[:, cut])
+                right = nn(lifted[...], w_right[:, cut])
                 grad = nt(rows_cot, w_down[cut, :])
                 hidden_units[2, place, cut] = (left * right).astype(BF16)
                 hidden_units[0, place, cut] = (grad * right).astype(BF16)
@@ -400,19 +381,20 @@
                 hidden_units[1, place, :], w_right[...]
             )
 
-            @pl.when(step < 2)
+            @pl.when(owned)
             def _():
                 grad_hidden[chunk(part), :] = back
 
-            @pl.when(step >= 2)
+            @pl.when(jnp.logical_not(owned))
             def _():
                 back_out[chunk(part), :] = back.astype(BF16)
                 back_copy(back_out, part).start()
 
             put_turned(turned.at[0], rows_in, place)
-            return carry
-
-        lax.fori_loop(0, 4, gated, 0)
+            put_turned(turned.at[1], rows_cot, place)
+            return carry
+
+        lax.fori_loop(0, blocks, gated, 0)
 
         def down_other(part, carry):
             down_out[chunk(part), :] = nn(
@@ -443,22 +425,25 @@
                 mixed_out[chunk(part), :] = for_peer.astype(BF16)
                 mixed_grad[at(own0 + part * BLOCK), :] = for_own.astype(BF16)
                 mixed_copy(part).start()
+                place = at(own0 + part * BLOCK)
                 both = jnp.sum(
-                    u_own[chunk(part), :].astype(F32) * for_own
-                    + u_in[chunk(part), :].astype(F32) * for_peer,
+                    u_all[place, :].astype(F32) * for_own + u_in[place, :].astype(F32) * for_peer,
                     axis=1,
                     keepdims=True,
                 )
                 lanes = to_rows(both)
-                for i in range(BLOCK // 128):
-                    cross[side, pl.ds(part * (BLOCK // 128) + i, 1), :] = lanes[i : i + 1, :]
+                for i in range(lanes_in):
+                    cross[side * 2 + part, i : i + 1, :] = lanes[i : i + 1, :]
+                cross_copy(part).start()
                 put_turned(low_turned, low, chunk(part))
+                scale = lane_column(scale_rows, side * 2 + part)
+                back_out[chunk(part), :width] = (u_all[place, :].astype(F32) * scale).astype(BF16)
+                back_out[chunk(part), width:] = (u_in[place, :].astype(F32) * scale).astype(BF16)
 
                 @pl.when(part == 1)
                 def _():
-                    over_x(10, cross.at[side], cross.at[side]).start()
-
-                down_copy(part).start()
+                    down_copy(0).start()
+                    down_copy(1).start()
 
             stage_core(
                 lhs, rhs, units, first, ffn_c.at[block], second_copy(0, block, ffn_c, ffn_y)
@@ -476,12 +461,13 @@
         lax.fori_loop(0, 2, down_own, 0)
         columns = 2 * width
         first = core_copy(3, 0, att_c, columns)
-        stage_send(low_turned, mixed, columns, first)
-        stage_core(low_turned, mixed, columns, first, att_c.at[0], second_copy(3, 0, att_c, att_y))
+        stage_send(low_turned, back_out, columns, first)
+        stage_core(low_turned, back_out, columns, first, att_c.at[0], second_copy(3, 0, att_c, att_y))
+        stage_second(0, 0, ffn_c, ffn_y, ffn_z)
 
     pl.run_scoped(
         middle,
-        pltpu.VMEM((half, features), BF16),
+        pltpu.VMEM((BLOCK, features), BF16),
         pltpu.VMEM((rows, features), BF16),
         pltpu.VMEM((2, features, rows), BF16),
         pltpu.VMEM((features, units), BF16),
@@ -490,7 +476,6 @@
         pltpu.VMEM((3, rows, units), BF16),
         pltpu.VMEM((half, features), BF16),
         pltpu.VMEM((features, half), BF16),
-        pltpu.VMEM((half, 2 * width), BF16),
     )
 
     def last(q_all, grads, k_all, v_all, slope_q, slope_k, heads_all, gate_all, pulls, weights, norm_out, norm_own, results, turned, tok_all):
@@ -517,25 +502,17 @@
             copy.wait()
         for part in range(2):
             mixed_copy(part).wait()
-        over_x(10, cross.at[side], cross.at[side]).wait()
-
-        def lane_rows(source, block):
-            return to_column(
-                jnp.concatenate(
-                    [source(block * (BLOCK // 128) + i) for i in range(BLOCK // 128)], axis=0
-                )
-            )
+            cross_copy(part).wait()
+
+        gain_row = jnp.concatenate([gain_lanes(i) for i in range(width // 128)], axis=1)
 
         def prepare(block, carry):
             place = chunk(block)
-            scale = lane_rows(lambda i: scale_rows[pl.ds(i, 1), :], block)
-            per_half = half // 128
-            joint = lane_rows(
-                lambda i: cross[lax.div(i, per_half), pl.ds(lax.rem(i, per_half), 1), :], block
-            )
+            scale = lane_column(scale_rows, block)
+            joint = lane_column(cross, block)
             grad = mixed_grad[place, :].astype(F32)
             head_rows = heads_all[place, :].astype(F32)
-            gain = gain_ref[0:1, :]
+            gain = gain_row
             scaled = grad * gate_all[place, :].astype(F32)
             unit = head_rows * scale
             gain_sum[0, 0:1, :] += jnp.sum(scaled * unit, axis=0, keepdims=True)
@@ -548,14 +525,7 @@
 
         lax.fori_loop(0, rows // BLOCK, prepare, 0)
         gain_copy(0, 0, sibling).start()
-
-        def seg_lanes(start, size):
-            return seg_ref[0:1, pl.ds(pl.multiple_of(start, 128), size)]
-
-        def seg_column(start):
-            return to_column(
-                jnp.concatenate([seg_lanes(start + i, 128) for i in range(0, BLOCK, 128)], axis=0)
-            )
+        stage_second(0, 1, ffn_c, ffn_y, ffn_z)
 
         def by_query(block, carry):
             place, span = chunk(block), pl.ds(pl.multiple_of(block * BLOCK, BLOCK), SPAN)
@@ -625,35 +595,6 @@
 
         lax.fori_loop(0, 4, normed_part, 0)
 
-        def turn(block, carry):
-            source = tok_all[chunk(block), :].astype(F32)
-            put_turned(turned, (source * rms_scale(source)).astype(BF16), chunk(block))
-            return carry
-
-        lax.fori_loop(0, rows // BLOCK, turn, 0)
-
-        gain_copy(0, 0, sibling).wait()
-        gain_sum[1] = gain_sum[0] + gain_in[0]
-        gain_copy(1, 1, beside).start()
-
-        def block_step(step, carry):
-            block = step + 1
-            rhs = pulls.at[step]
-            first = core_copy(3, block, att_c, columns)
-            stage_send(turned, rhs, columns, first)
-            stage_core(
-                turned, rhs, columns, first, att_c.at[block], second_copy(3, block, att_c, att_y)
-            )
-            return carry
-
-        lax.fori_loop(0, 2, block_step, 0)
-
-        def seconds(block, carry):
-            stage_second(0, block, ffn_c, ffn_y, ffn_z)
-            return carry
-
-        lax.fori_loop(0, 3, seconds, 0)
-
         def finish_out(part, carry):
             down_copy(part).wait()
             results[0, chunk(part), :] = (
@@ -666,6 +607,31 @@
             return carry
 
         lax.fori_loop(0, 2, finish_out, 0)
+        stage_second(0, 2, ffn_c, ffn_y, ffn_z)
+
+        def turn(block, carry):
+            source = tok_all[chunk(block), :].astype(F32)
+            put_turned(turned, (source * rms_scale(source)).astype(BF16), chunk(block))
+            return carry
+
+        lax.fori_loop(0, rows // BLOCK, turn, 0)
+
+        gain_copy(0, 0, sibling).wait()
+        gain_sum[1] = gain_sum[0] + gain_in[0]
+        gain_copy(1, 1, beside).start()
+
+        def block_step(step, carry):
+            block = step + 1
+            rhs = pulls.at[step]
+            first = core_copy(3, block, att_c, columns)
+            stage_send(turned, rhs, columns, first)
+            stage_core(
+                turned, rhs, columns, first, att_c.at[block], second_copy(3, block, att_c, att_y)
+            )
+            return carry
+
+        lax.fori_loop(0, 2, block_step, 0)
+
         gain_copy(1, 1, beside).wait()
         gain_sum[2] = gain_sum[1] + gain_in[1]
         for hop in range(1, thirds):
@@ -686,11 +652,13 @@
 
         lax.fori_loop(0, 2, finish_tokens, 0)
 
+        stage_second(3, 0, att_c, att_y, att_z)
+
         def seconds_last(block, carry):
             stage_second(3, block, att_c, att_y, att_z)
             return carry
 
-        lax.fori_loop(0, 3, seconds_last, 0)
+        lax.fori_loop(1, 3, seconds_last, 0)
 
         def ffn_total(block, carry):
             ffn_ref[block] = stage_third(0, block, ffn_y, ffn_z)
@@ -704,7 +672,7 @@
 
         lax.fori_loop(0, 1, attn_total, 0)
         turn_out[...] = attn_ref[0, :, width:]
-        turn_copy = over_x(19, turn_out, turn_in)
+        turn_copy = over_x(25, turn_out, turn_in)
         turn_copy.start()
         lax.fori_loop(1, 3, attn_total, 0)
         total = gain_sum[2]
@@ -748,48 +716,51 @@
     )
 
 
-def run_rest(ways, *args):
-    (seg, decays, sums, gain, tok, cot, u, wo, wo_part, wl) = args[:10]
+def run_layer(ways, *args):
+    (ids, decays, gain, tok, cot, wo, wl, wr, wd, wq) = args[:10]
     rows, features = tok.shape
-    width, units = u.shape[1], wl.shape[1]
+    width, units = wq.shape[1], wl.shape[1]
     half, thirds, share = rows // 2, ways // 4, features // ways
     quarter = features // 4
+    lane_rows = (rows // BLOCK, 8, 128)
     vmem = pl.BlockSpec(memory_space=pltpu.VMEM)
     hbm = pl.BlockSpec(memory_space=pl.ANY)
     shape = jax.ShapeDtypeStruct
     scratch = [
-        ((rows, features), BF16), ((half, width), BF16), ((width, features), BF16),
-        (sums.shape, F32), ((half, features), BF16), ((half, features), BF16),
-        ((rows, width), BF16), ((2, 8, 128), F32), ((half, features), BF16), ((share, width), F32),
+        ((rows, width), BF16), ((width, features), BF16), (lane_rows, F32),
+        ((half, features), BF16), ((half, features), BF16),
+        ((rows, width), BF16), (lane_rows, F32), ((half, features), BF16), ((share, width), F32),
         ((3, 2 * quarter, units), BF16), ((3, quarter, units), BF16),
         ((3, thirds - 1, share, units), BF16),
         ((3, 2 * quarter, 2 * width), BF16), ((3, quarter, 2 * width), BF16),
         ((3, thirds - 1, share, 2 * width), BF16), ((thirds + 1, 8, width), F32),
-        ((half, width), BF16), ((width, features), BF16), ((half, width), BF16),
+        ((1, rows + 2 * BAND), F32), (lane_rows, F32), ((rows, width), BF16),
+        ((width, features), BF16), ((half, width), BF16),
         ((half, features), BF16), ((half, features), F32), ((half, features), F32),
-        (sums.shape, F32), ((2 * quarter, max(units, 2 * width)), BF16), ((3, 8, width), F32),
+        (lane_rows, F32), ((2 * quarter, max(units, 2 * width)), BF16), ((3, 8, width), F32),
         ((share, width), F32),
     ]
     return pl.pallas_call(
-        functools.partial(rest, ways),
-        in_specs=[vmem, pl.BlockSpec(memory_space=pltpu.SMEM), vmem, vmem] + [hbm] * (len(args) - 4),
-        out_specs=[hbm, hbm, vmem, vmem, vmem],
+        functools.partial(layer, ways),
+        in_specs=[vmem, pl.BlockSpec(memory_space=pltpu.SMEM), vmem] + [hbm] * (len(args) - 3),
+        out_specs=[hbm, hbm, vmem, vmem, vmem] + [hbm] * 7,
         out_shape=[
             shape((rows, features), BF16), shape((rows, features), BF16),
             shape((3, share, units), F32), shape((3, share, 2 * width), F32), shape((8, width), F32),
-        ],
+        ]
+        + [shape((rows, width), BF16)] * 7,
         scratch_shapes=[pltpu.VMEM(size, dtype) for size, dtype in scratch]
         + [
-            pltpu.SemaphoreType.DMA((20,)), pltpu.SemaphoreType.DMA((20,)),
+            pltpu.SemaphoreType.DMA((26,)), pltpu.SemaphoreType.DMA((26,)),
             pltpu.SemaphoreType.DMA((2, 6)), pltpu.SemaphoreType.DMA((2, 6)),
             pltpu.SemaphoreType.DMA((7, thirds + 1)), pltpu.SemaphoreType.DMA((7, thirds + 1)),
-            pltpu.SemaphoreType.DMA((12,)),
+            pltpu.SemaphoreType.DMA((12,)), pltpu.SemaphoreType.DMA((7,)),
         ],
         compiler_params=pltpu.CompilerParams(
             collective_id=1, has_side_effects=True, vmem_limit_bytes=VMEM_LIMIT
         ),
         cost_estimate=pl.CostEstimate(flops=5 * 10**10, bytes_accessed=60 * 2**20, transcendentals=10**6),
-        name="rest",
+        name="layer",
     )(*args)
 
 
@@ -799,21 +770,10 @@
 ):
     heads_here, head_size = norm_gain.shape
     width = heads_here * head_size
-    gain = norm_gain.astype(F32).reshape(1, width)
-    segments = jnp.pad(
-        segment_ids.astype(F32).reshape(1, -1), ((0, 0), (BAND, BAND)), constant_values=-1.0
-    )
-    core = lax.rem(lax.axis_index("dp"), 2)
-    part = lax.dynamic_slice_in_dim(output_weight, core * (width // 2), width // 2, 0)
-    part = lax.ppermute(part, "tensor", [(0, 1), (1, 0)])
-    u, heads, gate, q, k, v, sq, sk, sums = run_attend(
-        segments, decay_rate, tokens, query_weight, key_weight, value_weight, gate_weight, gain
-    )
-    block_out, tokens_grad, ffn, attn, gain_total = run_rest(
-        ways, segments, decay_rate, sums, gain, tokens, cotangent, u, output_weight, part,
+    block_out, tokens_grad, ffn, attn, gain_total = run_layer(
+        ways, segment_ids, decay_rate, norm_gain, tokens, cotangent, output_weight,
         left_weight, right_weight, down_weight, query_weight, key_weight, value_weight, gate_weight,
-        heads, gate, q, k, v, sq, sk,
-    )
+    )[:5]
     each = head_size // ways
     gain_grad = lax.dynamic_slice_in_dim(
         gain_total[0].reshape(heads_here, head_size), lax.axis_index("dp") * each, each, 1

time: 236 us -> 189 us (0.80)
  Pallas kernels: 218 us -> 179 us
  local copies, waits for them, and re-layouts: 9.52 us -> 4.57 us
  starting transfers between devices: 3 us -> 0 us
    pallas_call x2 -> x1, Pallas kernels: 218 us -> 179 us  [run_layer(): pl.pallas_call(functools.partial(layer, ways), in_specs=[vmem, pl.BlockSp...]
    ppermute x1 -> x0, starting transfers between devices: 3 us -> none  [local(): part = lax.ppermute(part, 'tensor', [(0, 1), (1, 0)])]
  transfers between devices with their start and end apart: 1 -> 0, of which waited for: 0 -> 0; matrix products, arithmetic and copies ran while one was open for 1% -> 0% of each run, Pallas kernels for 6% -> 0%
where the time goes in v3:
time: 189 us; the launch traced here: 188 us
  Pallas kernels  179 us (95%)
  local copies, waits for them, and re-layouts  4.57 us (2%)
  other arithmetic  4.2 us (2%)
    pallas_call x1, Pallas kernels, run_layer(): pl.pallas_call(functools.partial(layer, ways), in_specs=[vmem, pl.BlockSp...  179 us
    convert_element_type x1, other arithmetic, local(): tokens_grad.astype(F32)  4.2 us

profile of v3, /device:TPU:0, one launch (start us, length us, event | category | flops | bytes accessed | tf_op | source)
XLA Modules:
  0.0 188.3 jit_solution(3505072977125084955)
XLA Ops:
  0.6 178.9 %layer.1 = (bf16[1024,1024]{1,0:T(8,128)(2,1)}, bf16[1024,1024]{1,0:T(8,128)(2,1)}, f32[3,64,1408]{2,1,0:T(8,128)}, f32[3,64,1024]{2,1,0:T(8,128)}, f32[8,512]{1...) custom-call(s32[1,1024]{1,0:T(1,128)} %ids_ref.1, ...), custom_call_target="tpu_custom_call" | custom-call | flops 49999998976 | bytes 62914560 | tf_op jit(solution)/shard_map/layer/pallas_call | solution.py:743
  179.6 0.0 copy-start.2
  179.6 0.0 copy-start.1
  179.6 4.2 %convert_element_type.3 = f32[1024,1024]{1,0:T(8,128)} convert(bf16[1024,1024]{1,0:T(8,128)(2,1)} %get-tuple-element.17) | non-fusion elementwise | flops 1048576 | bytes 6291456 | tf_op jit(solution)/shard_map/convert_element_type | solution.py:783
  183.8 0.0 copy-start
  183.8 0.0 copy-done.2
  183.8 0.8 slice_bitcast_fusion.3
  184.6 0.8 slice.32
  185.4 0.7 constant_dynamic-slice_fusion
  186.0 0.0 copy-done.1
  186.0 1.0 slice_bitcast_fusion
  187.0 0.0 copy-done
  187.0 1.3 copy.25
Async XLA Ops:
  179.6 4.2 %copy-start.2 = (f32[3,64,1024]{2,1,0:T(8,128)S(1)}, f32[3,64,1024]{2,1,0:T(8,128)}, u32[]{:S(2)}) copy-start(f32[3,64,1024]{2,1,0:T(8,128)} %get-tuple-element.18) | copy-start | bytes 2359300
  179.6 6.5 %copy-start.1 = (f32[3,64,1408]{2,1,0:T(8,128)S(1)}, f32[3,64,1408]{2,1,0:T(8,128)}, u32[]{:S(2)}) copy-start(f32[3,64,1408]{2,1,0:T(8,128)} %get-tuple-element.20) | copy-start | bytes 3244036
  183.8 3.2 %copy-start = (bf16[1024,1024]{1,0:T(8,128)(2,1)S(1)}, bf16[1024,1024]{1,0:T(8,128)(2,1)}, u32[]{:S(2)}) copy-start(bf16[1024,1024]{1,0:T(8,128)(2,1)} %get-tuple-element.40) | copy-start | bytes 6291460

commit v4 on v3

--- a/solution.py
+++ b/solution.py
@@ -450,7 +450,12 @@
             )
             return carry
 
-        lax.fori_loop(0, 3, block_step, 0)
+        lax.fori_loop(0, 2, block_step, 0)
+        columns = 2 * width
+        first = core_copy(3, 0, att_c, columns)
+        stage_send(low_turned, back_out, columns, first)
+        stage_core(low_turned, back_out, columns, first, att_c.at[0], second_copy(3, 0, att_c, att_y))
+        lax.fori_loop(2, 3, block_step, 0)
 
         def down_own(part, carry):
             hidden[chunk(part), :] += nn(
@@ -459,10 +464,6 @@
             return carry
 
         lax.fori_loop(0, 2, down_own, 0)
-        columns = 2 * width
-        first = core_copy(3, 0, att_c, columns)
-        stage_send(low_turned, back_out, columns, first)
-        stage_core(low_turned, back_out, columns, first, att_c.at[0], second_copy(3, 0, att_c, att_y))
         stage_second(0, 0, ffn_c, ffn_y, ffn_z)
 
     pl.run_scoped(
@@ -545,7 +546,19 @@
                 ).astype(BF16)
             return carry
 
+        def finish_out(part, carry):
+            down_copy(part).wait()
+            results[0, chunk(part), :] = (
+                hidden[chunk(part), :] + down_in[chunk(part), :].astype(F32)
+            ).astype(BF16)
+            out_copy(results.at[0], part).start()
+            pltpu.make_async_copy(
+                results.at[0, chunk(part), :], out_ref.at[at(own0 + part * BLOCK), :], local.at[part]
+            ).start()
+            return carry
+
         lax.fori_loop(0, rows // BLOCK, by_query, 0)
+        lax.fori_loop(0, 1, finish_out, 0)
 
         def by_key(block, carry):
             place, span = chunk(block), pl.ds(pl.multiple_of(block * BLOCK, BLOCK), SPAN)
@@ -572,6 +585,8 @@
             return carry
 
         lax.fori_loop(0, rows // BLOCK, by_key, 0)
+        lax.fori_loop(1, 2, finish_out, 0)
+        stage_second(3, 0, att_c, att_y, att_z)
         for copy in later:
             copy.wait()
 
@@ -595,19 +610,6 @@
 
         lax.fori_loop(0, 4, normed_part, 0)
 
-        def finish_out(part, carry):
-            down_copy(part).wait()
-            results[0, chunk(part), :] = (
-                hidden[chunk(part), :] + down_in[chunk(part), :].astype(F32)
-            ).astype(BF16)
-            out_copy(results.at[0], part).start()
-            pltpu.make_async_copy(
-                results.at[0, chunk(part), :], out_ref.at[at(own0 + part * BLOCK), :], local.at[part]
-            ).start()
-            return carry
-
-        lax.fori_loop(0, 2, finish_out, 0)
-        stage_second(0, 2, ffn_c, ffn_y, ffn_z)
 
         def turn(block, carry):
             source = tok_all[chunk(block), :].astype(F32)
@@ -628,14 +630,27 @@
             stage_core(
                 turned, rhs, columns, first, att_c.at[block], second_copy(3, block, att_c, att_y)
             )
+
+            @pl.when(step == 0)
+            def _():
+                stage_second(0, 2, ffn_c, ffn_y, ffn_z)
+
             return carry
 
         lax.fori_loop(0, 2, block_step, 0)
-
         gain_copy(1, 1, beside).wait()
         gain_sum[2] = gain_sum[1] + gain_in[1]
         for hop in range(1, thirds):
             gain_copy(2, 1 + hop, far(hop)).start()
+
+        def attn_total(block, carry):
+            attn_ref[block] = stage_third(3, block, att_y, att_z)
+            return carry
+
+        lax.fori_loop(0, 1, attn_total, 0)
+        turn_out[...] = attn_ref[0, :, width:]
+        turn_copy = over_x(25, turn_out, turn_in)
+        turn_copy.start()
 
         def finish_tokens(part, carry):
             norm_copy(norm_out, part).wait()
@@ -652,8 +667,6 @@
 
         lax.fori_loop(0, 2, finish_tokens, 0)
 
-        stage_second(3, 0, att_c, att_y, att_z)
-
         def seconds_last(block, carry):
             stage_second(3, block, att_c, att_y, att_z)
             return carry
@@ -665,15 +678,6 @@
             return carry
 
         lax.fori_loop(0, 3, ffn_total, 0)
-
-        def attn_total(block, carry):
-            attn_ref[block] = stage_third(3, block, att_y, att_z)
-            return carry
-
-        lax.fori_loop(0, 1, attn_total, 0)
-        turn_out[...] = attn_ref[0, :, width:]
-        turn_copy = over_x(25, turn_out, turn_in)
-        turn_copy.start()
         lax.fori_loop(1, 3, attn_total, 0)
         total = gain_sum[2]
         for hop in range(1, thirds):
@@ -764,33 +768,93 @@
     )(*args)
 
 
+def finish(
+    ways, out_in, tg_in, ffn, attn, gain_in,
+    out, tg, query, key, value, gate, output, gain, left, right, down,
+    out_held, tg_low, tg_wide, ffn_held, attn_held, arrived, left_here,
+):
+    width = query.shape[1]
+    blocks = tg.shape[0] // BLOCK
+    pairs = []
+    for i in range(blocks):
+        place = at(i * BLOCK)
+        pairs.append((tg_in.at[place, :], tg_low.at[place, :], tg_wide.at[place, :], tg.at[place, :]))
+    for i, target in enumerate((left, right, down)):
+        pairs.append((ffn.at[i], ffn_held.at[i], ffn_held.at[i], target))
+    for i, j, target in ((1, 0, query), (1, 1, key), (2, 0, value), (2, 1, gate), (0, 0, output)):
+        cut = pl.ds(j * width, width)
+        held = attn_held.at[i, :, cut]
+        pairs.append((attn.at[i, :, cut], held, held, target))
+    for i in range(blocks):
+        place = at(i * BLOCK)
+        pairs.append((out_in.at[place, :], out_held.at[place, :], out_held.at[place, :], out.at[place, :]))
+    loads = [
+        pltpu.make_async_copy(source, held, arrived.at[i])
+        for i, (source, held, _, _) in enumerate(pairs)
+    ]
+    stores = [
+        pltpu.make_async_copy(held, target, left_here.at[i])
+        for i, (_, _, held, target) in enumerate(pairs)
+    ]
+    for copy in loads:
+        copy.start()
+    heads, each = gain.shape
+    rows_in = jnp.concatenate([gain_in[0:1, i * 128 : i * 128 + 128] for i in range(heads)], axis=0)
+    lane = lax.broadcasted_iota(jnp.int32, rows_in.shape, 1)
+    place = lax.broadcasted_iota(jnp.int32, gain.shape, 1)
+    first = lax.axis_index("dp") * each
+    found = jnp.zeros(gain.shape, F32)
+    for i in range(each):
+        column = jnp.sum(jnp.where(lane == first + i, rows_in, 0.0), axis=1, keepdims=True)
+        found = jnp.where(place == i, column, found)
+    gain[...] = found
+    for i in range(len(pairs)):
+        loads[i].wait()
+        if i < blocks:
+            tg_wide[at(i * BLOCK), :] = tg_low[at(i * BLOCK), :].astype(F32)
+        stores[i].start()
+    for copy in stores:
+        copy.wait()
+
+
+def run_finish(ways, heads, out_in, tg_in, ffn, attn, gain_in):
+    rows, features = tg_in.shape
+    share, units, width = ffn.shape[1], ffn.shape[2], attn.shape[2] // 2
+    vmem = pl.BlockSpec(memory_space=pltpu.VMEM)
+    hbm = pl.BlockSpec(memory_space=pl.ANY)
+    shape = lambda *size: jax.ShapeDtypeStruct(size, F32)
+    copies = 2 * (rows // BLOCK) + 8
+    return pl.pallas_call(
+        functools.partial(finish, ways),
+        in_specs=[hbm] * 4 + [vmem],
+        out_specs=[hbm] * 7 + [vmem] + [hbm] * 3,
+        out_shape=[jax.ShapeDtypeStruct((rows, features), BF16), shape(rows, features)]
+        + [shape(share, width)] * 5
+        + [shape(heads, gain_in.shape[1] // heads // ways)]
+        + [shape(share, units)] * 3,
+        scratch_shapes=[
+            pltpu.VMEM((rows, features), BF16), pltpu.VMEM((rows, features), BF16),
+            pltpu.VMEM((rows, features), F32), pltpu.VMEM((3, share, units), F32),
+            pltpu.VMEM((3, share, 2 * width), F32),
+            pltpu.SemaphoreType.DMA((copies,)), pltpu.SemaphoreType.DMA((copies,)),
+        ],
+        compiler_params=pltpu.CompilerParams(vmem_limit_bytes=VMEM_LIMIT),
+        name="finish",
+    )(out_in, tg_in, ffn, attn, gain_in)
+
+
 def local(
     ways, tokens, segment_ids, decay_rate, query_weight, key_weight, value_weight, gate_weight,
     output_weight, norm_gain, left_weight, right_weight, down_weight, cotangent,
 ):
-    heads_here, head_size = norm_gain.shape
-    width = heads_here * head_size
-    block_out, tokens_grad, ffn, attn, gain_total = run_layer(
+    held = run_layer(
         ways, segment_ids, decay_rate, norm_gain, tokens, cotangent, output_weight,
         left_weight, right_weight, down_weight, query_weight, key_weight, value_weight, gate_weight,
     )[:5]
-    each = head_size // ways
-    gain_grad = lax.dynamic_slice_in_dim(
-        gain_total[0].reshape(heads_here, head_size), lax.axis_index("dp") * each, each, 1
-    )
-    return (
-        block_out,
-        tokens_grad.astype(F32),
-        attn[1, :, :width],
-        attn[1, :, width:],
-        attn[2, :, :width],
-        attn[2, :, width:],
-        attn[0, :, :width].T,
-        gain_grad,
-        ffn[0],
-        ffn[1],
-        ffn[2].T,
-    )
+    results = list(run_finish(ways, norm_gain.shape[0], *held))
+    for turned in (6, 10):
+        results[turned] = results[turned].T
+    return tuple(results)
 
 
 def solution(mesh):

time: 189 us -> 177 us (0.937)
  local copies, waits for them, and re-layouts: 4.57 us -> 0 us
  other arithmetic: 4.2 us -> 0 us
  Pallas kernels: 179 us -> 176 us
    pallas_call x1, Pallas kernels: 179 us -> 169 us  [run_layer(): pl.pallas_call(functools.partial(layer, ways), in_specs=[vmem, pl.BlockSp...]
    pallas_call x0 -> x1, Pallas kernels: none -> 6.65 us  [run_finish(): pl.pallas_call(functools.partial(finish, ways), in_specs=[hbm] * 4 + [vme...]
    convert_element_type x1 -> x0, other arithmetic: 4.2 us -> none  [local(): tokens_grad.astype(F32)]
where the time goes in v4:
time: 177 us
  Pallas kernels  176 us (99%)
    pallas_call x1, Pallas kernels, run_layer(): pl.pallas_call(functools.partial(layer, ways), in_specs=[vmem, pl.BlockSp...  169 us
    pallas_call x1, Pallas kernels, run_finish(): pl.pallas_call(functools.partial(finish, ways), in_specs=[hbm] * 4 + [vme...  6.65 us

profile of v4, /device:TPU:0, one launch (start us, length us, event | category | flops | bytes accessed | tf_op | source)
XLA Modules:
  0.0 176.6 jit_solution(15045004300307217619)
XLA Ops:
  0.6 169.2 %layer.1 = (bf16[1024,1024]{1,0:T(8,128)(2,1)}, bf16[1024,1024]{1,0:T(8,128)(2,1)}, f32[3,64,1408]{2,1,0:T(8,128)}, f32[3,64,1024]{2,1,0:T(8,128)}, f32[8,512]{1...) custom-call(s32[1,1024]{1,0:T(1,128)} %ids_ref.1, ...), custom_call_target="tpu_custom_call" | custom-call | flops 49999998976 | bytes 62914560 | tf_op jit(solution)/shard_map/layer/pallas_call | solution.py:747
  169.8 6.6 %finish.1 = (bf16[1024,1024]{1,0:T(8,128)(2,1)}, f32[1024,1024]{1,0:T(8,128)}, f32[64,512]{1,0:T(8,128)}, f32[64,512]{1,0:T(8,128)}, f32[64,512]{1,0:T(8,128)}, ...) custom-call(bf16[1024,1024]{1,0:T(8,128)(2,1)} %get-tuple-element.27, ...), custom_call_target="tpu_custom_call" | custom-call | tf_op jit(solution)/shard_map/finish/pallas_call | solution.py:827

commit v5 on v4

--- a/solution.py
+++ b/solution.py
@@ -73,7 +73,7 @@
 def layer(
     ways,
     ids_ref, decay_ref, gain_ref, tok, cot, wo, wl, wr, wd, wq, wk, wv, wg,
-    out_ref, tg_ref, ffn_ref, attn_ref, gain_out,
+    out_ref, tg_ref, ffn_out, attn_out, gain_out,
     q, k, v, gate, heads, sq, sk,
     u_in, wo_peer, sum_in, back_in, down_in, mixed_grad, cross, norm_in, turn_in,
     ffn_c, ffn_y, ffn_z, att_c, att_y, att_z, gain_in,
@@ -152,20 +152,29 @@
     def tg_copy(source, part):
         return over_x(23 + part, source.at[chunk(part), :], tg_ref.at[at(own0 + part * BLOCK), :])
 
-    slice_rows = width // 4
-    wo_start = core * (2 * slice_rows) + second * slice_rows
-    wo_piece = pl.ds(pl.multiple_of(wo_start, slice_rows), slice_rows)
+    odd = lax.rem(third, 2)
+    paired = ((third + 1 - 2 * odd) * 4 + second * 2 + core, side)
+
+    def wo_rows(start, size):
+        return pl.ds(pl.multiple_of(start, size), size)
 
     def wo_across():
-        return over_x(8, wo.at[wo_piece, :], wo_peer.at[wo_piece, :])
+        place = wo_rows(((core * 2 + second) * 2 + odd) * (width // 8), width // 8)
+        return over_x(8, wo.at[place, :], wo_peer.at[place, :])
+
+    def wo_pass(index, place, device):
+        piece = wo_peer.at[place, :]
+        return remote(piece, piece, send.at[index], recv.at[index], device)
+
+    def wo_paired():
+        place = wo_rows(((core * 2 + second) * 2 + odd) * (width // 8), width // 8)
+        return wo_pass(26, place, paired)
 
     def wo_beside():
-        piece = wo_peer.at[wo_piece, :]
-        return remote(piece, piece, send.at[9], recv.at[9], beside)
+        return wo_pass(9, wo_rows((core * 2 + second) * (width // 4), width // 4), beside)
 
     def wo_sibling():
-        piece = wo_peer.at[pl.ds(pl.multiple_of(core * (2 * slice_rows), 2 * slice_rows), 2 * slice_rows), :]
-        return remote(piece, piece, send.at[10], recv.at[10], sibling)
+        return wo_pass(10, wo_rows(core * (width // 2), width // 2), sibling)
 
     def core_copy(first, block, landing, columns):
         return remote(
@@ -328,9 +337,14 @@
                     source.at[place, :], target.at[place, :], kept.at[index]
                 ).start()
 
+            @pl.when(block == 0)
+            def _():
+                wo_across().wait()
+                wo_paired().start()
+
             @pl.when(block == 1)
             def _():
-                wo_across().wait()
+                wo_paired().wait()
                 wo_beside().start()
 
             @pl.when(block == blocks - 1)
@@ -479,7 +493,7 @@
         pltpu.VMEM((features, half), BF16),
     )
 
-    def last(q_all, grads, k_all, v_all, slope_q, slope_k, heads_all, gate_all, pulls, weights, norm_out, norm_own, results, turned, tok_all):
+    def last(q_all, grads, k_all, v_all, slope_q, slope_k, heads_all, gate_all, pulls, weights, norm_out, norm_own, results, turned, tok_all, ffn_ref, attn_ref):
         columns = 2 * width
         loads = [
             load(0, v, v_all.at[pl.ds(BAND, rows), :]),
@@ -643,12 +657,20 @@
         for hop in range(1, thirds):
             gain_copy(2, 1 + hop, far(hop)).start()
 
+        def attn_copy(block):
+            return pltpu.make_async_copy(attn_ref.at[block], attn_out.at[block], local.at[7 + block])
+
         def attn_total(block, carry):
             attn_ref[block] = stage_third(3, block, att_y, att_z)
+
+            @pl.when(block > 0)
+            def _():
+                attn_copy(block).start()
+
             return carry
 
         lax.fori_loop(0, 1, attn_total, 0)
-        turn_out[...] = attn_ref[0, :, width:]
+        turn_out[...] = attn_ref[0, :, width:].astype(BF16)
         turn_copy = over_x(25, turn_out, turn_in)
         turn_copy.start()
 
@@ -675,6 +697,7 @@
 
         def ffn_total(block, carry):
             ffn_ref[block] = stage_third(0, block, ffn_y, ffn_z)
+            pltpu.make_async_copy(ffn_ref.at[block], ffn_out.at[block], local.at[4 + block]).start()
             return carry
 
         lax.fori_loop(0, 3, ffn_total, 0)
@@ -685,7 +708,8 @@
             total = total + gain_in[1 + hop]
         gain_out[...] = total
         turn_copy.wait()
-        attn_ref[0, :, :width] += turn_in[...]
+        attn_ref[0, :, :width] += turn_in[...].astype(F32)
+        attn_copy(0).start()
 
         def close(part, carry):
             out_copy(results.at[0], part).wait()
@@ -699,6 +723,9 @@
             return carry
 
         lax.fori_loop(0, 2, close, 0)
+        for block in range(3):
+            pltpu.make_async_copy(ffn_ref.at[block], ffn_out.at[block], local.at[4 + block]).wait()
+            attn_copy(block).wait()
 
     pl.run_scoped(
         last,
@@ -717,6 +744,8 @@
         pltpu.VMEM((2, half, features), BF16),
         pltpu.VMEM((features, rows), BF16),
         pltpu.VMEM((rows, features), BF16),
+        pltpu.VMEM(ffn_out.shape, F32),
+        pltpu.VMEM(attn_out.shape, F32),
     )
 
 
@@ -733,7 +762,7 @@
     scratch = [
         ((rows, width), BF16), ((width, features), BF16), (lane_rows, F32),
         ((half, features), BF16), ((half, features), BF16),
-        ((rows, width), BF16), (lane_rows, F32), ((half, features), BF16), ((share, width), F32),
+        ((rows, width), BF16), (lane_rows, F32), ((half, features), BF16), ((share, width), BF16),
         ((3, 2 * quarter, units), BF16), ((3, quarter, units), BF16),
         ((3, thirds - 1, share, units), BF16),
         ((3, 2 * quarter, 2 * width), BF16), ((3, quarter, 2 * width), BF16),
@@ -742,12 +771,12 @@
         ((width, features), BF16), ((half, width), BF16),
         ((half, features), BF16), ((half, features), F32), ((half, features), F32),
         (lane_rows, F32), ((2 * quarter, max(units, 2 * width)), BF16), ((3, 8, width), F32),
-        ((share, width), F32),
+        ((share, width), BF16),
     ]
     return pl.pallas_call(
         functools.partial(layer, ways),
         in_specs=[vmem, pl.BlockSpec(memory_space=pltpu.SMEM), vmem] + [hbm] * (len(args) - 3),
-        out_specs=[hbm, hbm, vmem, vmem, vmem] + [hbm] * 7,
+        out_specs=[hbm] * 4 + [vmem] + [hbm] * 7,
         out_shape=[
             shape((rows, features), BF16), shape((rows, features), BF16),
             shape((3, share, units), F32), shape((3, share, 2 * width), F32), shape((8, width), F32),
@@ -755,7 +784,7 @@
         + [shape((rows, width), BF16)] * 7,
         scratch_shapes=[pltpu.VMEM(size, dtype) for size, dtype in scratch]
         + [
-            pltpu.SemaphoreType.DMA((26,)), pltpu.SemaphoreType.DMA((26,)),
+            pltpu.SemaphoreType.DMA((27,)), pltpu.SemaphoreType.DMA((27,)),
             pltpu.SemaphoreType.DMA((2, 6)), pltpu.SemaphoreType.DMA((2, 6)),
             pltpu.SemaphoreType.DMA((7, thirds + 1)), pltpu.SemaphoreType.DMA((7, thirds + 1)),
             pltpu.SemaphoreType.DMA((12,)), pltpu.SemaphoreType.DMA((7,)),
@@ -774,20 +803,17 @@
     out_held, tg_low, tg_wide, ffn_held, attn_held, arrived, left_here,
 ):
     width = query.shape[1]
-    blocks = tg.shape[0] // BLOCK
-    pairs = []
-    for i in range(blocks):
-        place = at(i * BLOCK)
-        pairs.append((tg_in.at[place, :], tg_low.at[place, :], tg_wide.at[place, :], tg.at[place, :]))
+    blocks = 2
+    size = tg.shape[0] // blocks
+    places = [pl.ds(i * size, size) for i in range(blocks)]
+    pairs = [(tg_in.at[i, :], tg_low.at[i, :], tg_wide.at[i, :], tg.at[i, :]) for i in places]
+    pairs += [(out_in.at[i, :], out_held.at[i, :], out_held.at[i, :], out.at[i, :]) for i in places]
     for i, target in enumerate((left, right, down)):
         pairs.append((ffn.at[i], ffn_held.at[i], ffn_held.at[i], target))
     for i, j, target in ((1, 0, query), (1, 1, key), (2, 0, value), (2, 1, gate), (0, 0, output)):
         cut = pl.ds(j * width, width)
         held = attn_held.at[i, :, cut]
         pairs.append((attn.at[i, :, cut], held, held, target))
-    for i in range(blocks):
-        place = at(i * BLOCK)
-        pairs.append((out_in.at[place, :], out_held.at[place, :], out_held.at[place, :], out.at[place, :]))
     loads = [
         pltpu.make_async_copy(source, held, arrived.at[i])
         for i, (source, held, _, _) in enumerate(pairs)
@@ -811,7 +837,7 @@
     for i in range(len(pairs)):
         loads[i].wait()
         if i < blocks:
-            tg_wide[at(i * BLOCK), :] = tg_low[at(i * BLOCK), :].astype(F32)
+            tg_wide[places[i], :] = tg_low[places[i], :].astype(F32)
         stores[i].start()
     for copy in stores:
         copy.wait()
@@ -823,7 +849,7 @@
     vmem = pl.BlockSpec(memory_space=pltpu.VMEM)
     hbm = pl.BlockSpec(memory_space=pl.ANY)
     shape = lambda *size: jax.ShapeDtypeStruct(size, F32)
-    copies = 2 * (rows // BLOCK) + 8
+    copies = 12
     return pl.pallas_call(
         functools.partial(finish, ways),
         in_specs=[hbm] * 4 + [vmem],

time: 177 us -> 172 us (0.972)
  Pallas kernels: 176 us -> 170 us
    pallas_call x1, Pallas kernels: 169 us -> 164 us  [run_layer(): pl.pallas_call(functools.partial(layer, ways), in_specs=[vmem, pl.BlockSp...]
where the time goes in v5:
time: 172 us; the launch traced here: 171 us
  Pallas kernels  170 us (99%)
    pallas_call x1, Pallas kernels, run_layer(): pl.pallas_call(functools.partial(layer, ways), in_specs=[vmem, pl.BlockSp...  164 us
    pallas_call x1, Pallas kernels, run_finish(): pl.pallas_call(functools.partial(finish, ways), in_specs=[hbm] * 4 + [vme...  6.02 us

profile of v5, /device:TPU:0, one launch (start us, length us, event | category | flops | bytes accessed | tf_op | source)
XLA Modules:
  0.0 171.3 jit_solution(827834698283997813)
XLA Ops:
  0.6 164.4 %layer.1 = (bf16[1024,1024]{1,0:T(8,128)(2,1)}, bf16[1024,1024]{1,0:T(8,128)(2,1)}, f32[3,64,1408]{2,1,0:T(8,128)}, f32[3,64,1024]{2,1,0:T(8,128)}, f32[8,512]{1...) custom-call(s32[1,1024]{1,0:T(1,128)} %ids_ref.1, ...), custom_call_target="tpu_custom_call" | custom-call | flops 49999998976 | bytes 62914560 | tf_op jit(solution)/shard_map/layer/pallas_call | solution.py:776
  165.1 6.0 %finish.1 = (bf16[1024,1024]{1,0:T(8,128)(2,1)}, f32[1024,1024]{1,0:T(8,128)}, f32[64,512]{1,0:T(8,128)}, f32[64,512]{1,0:T(8,128)}, f32[64,512]{1,0:T(8,128)}, ...) custom-call(bf16[1024,1024]{1,0:T(8,128)(2,1)} %get-tuple-element.27, ...), custom_call_target="tpu_custom_call" | custom-call | tf_op jit(solution)/shard_map/finish/pallas_call | solution.py:853

commit v6 on v5

--- a/solution.py
+++ b/solution.py
@@ -114,7 +114,9 @@
     def put_turned(target, block, column):
         turned = jnp.transpose(block)
         for owner in range(ways):
-            place = (owner % 2) * (ways // 2) + (owner // 2 % 2) * (ways // 4) + owner // 4
+            place, left = 0, owner
+            for _ in range(ways.bit_length() - 1):
+                place, left = place * 2 + left % 2, left // 2
             target[place * share : (place + 1) * share, column] = turned[
                 owner * share : (owner + 1) * share, :
             ]
@@ -176,50 +178,77 @@
     def wo_sibling():
         return wo_pass(10, wo_rows(core * (width // 2), width // 2), sibling)
 
-    def core_copy(first, block, landing, columns):
+    def section(part):
+        return chunk(1 - second + part * (2 * second - 1))
+
+    def core_copy(first, block, landing, columns, part):
         return remote(
-            core_out.at[:, pl.ds(0, columns)], landing.at[block],
-            dp_send.at[0, first + block], dp_recv.at[0, first + block], sibling,
+            core_out.at[section(part), pl.ds(0, columns)], landing.at[block, section(part), :],
+            dp_send.at[part, first + block], dp_recv.at[part, first + block], sibling,
         )
 
     def second_copy(first, block, summed, landing):
         return remote(
             summed.at[block, at((1 - second) * BLOCK), :], landing.at[block],
-            dp_send.at[1, first + block], dp_recv.at[1, first + block], beside,
+            dp_send.at[2, first + block], dp_recv.at[2, first + block], beside,
         )
 
-    def third_copy(first, block, hop, summed, landing):
-        piece = pl.ds(pl.multiple_of(lax.rem(third + hop, thirds) * share, share), share)
+    levels = thirds.bit_length() - 1
+
+    def third_bit(level):
+        return lax.rem(lax.div(third, 2**level), 2)
+
+    def third_start(level):
+        return BLOCK - (BLOCK >> level)
+
+    def third_rows(level, bit):
+        size = BLOCK >> (level + 1)
+        start = bit * size + (third_start(level - 1) if level else 0)
+        return pl.ds(pl.multiple_of(start, size), size)
+
+    def third_source(level, summed, landing):
+        return landing if level else summed
+
+    def third_copy(first, block, level, summed, landing):
+        bit = third_bit(level)
+        other = third + (1 - 2 * bit) * 2**level
         return remote(
-            summed.at[block, piece, :], landing.at[block, hop - 1],
-            z_send.at[first + block, hop - 1], z_recv.at[first + block, hop - 1], far(hop),
+            third_source(level, summed, landing).at[block, third_rows(level, 1 - bit), :],
+            landing.at[block, pl.ds(third_start(level), BLOCK >> (level + 1)), :],
+            z_send.at[first + block, level], z_recv.at[first + block, level],
+            (other * 4 + second * 2 + core, side),
         )
 
-    def stage_send(turned, grads, columns, copy):
+    def stage_send(turned, grads, first, block, landing, columns):
         def one(part, carry):
-            left_op = turned[at((1 - core) * 2 * BLOCK + part * BLOCK), :]
+            place = section(part)
+            left_op = turned[pl.ds(pl.multiple_of((1 - core) * 2 * BLOCK + place.start, BLOCK), BLOCK), :]
             for start, size in tiles(columns):
-                core_out[chunk(part), start : start + size] = nn(
+                core_out[place, start : start + size] = nn(
                     left_op, grads[:, start : start + size]
                 ).astype(BF16)
+            core_copy(first, block, landing, columns, part).start()
             return carry
 
         lax.fori_loop(0, 2, one, 0)
-        copy.start()
-
-    def stage_core(turned, grads, columns, copy, landing, onward):
-        copy.wait()
-
+
+    def stage_core(turned, grads, first, block, landing, columns, onward):
         def one(part, carry):
-            left_op = turned[at(core * 2 * BLOCK + part * BLOCK), :]
+            place = section(part)
+            left_op = turned[pl.ds(pl.multiple_of(core * 2 * BLOCK + place.start, BLOCK), BLOCK), :]
+            core_copy(first, block, landing, columns, part).wait()
             for start, size in tiles(columns):
                 cut = slice(start, start + size)
-                total = nn(left_op, grads[:, cut]) + landing[chunk(part), cut].astype(F32)
-                landing[chunk(part), cut] = total.astype(BF16)
+                total = nn(left_op, grads[:, cut]) + landing[block, place, cut].astype(F32)
+                landing[block, place, cut] = total.astype(BF16)
+
+            @pl.when(part == 0)
+            def _():
+                onward.start()
+
             return carry
 
         lax.fori_loop(0, 2, one, 0)
-        onward.start()
 
     def stage_second(first, block, summed, landing, group_out):
         copy = second_copy(first, block, summed, landing)
@@ -231,16 +260,24 @@
                 + landing[block, :, cut].astype(F32)
             )
             landing[block, :, cut] = total.astype(BF16)
-        for hop in range(1, thirds):
-            third_copy(first, block, hop, landing, group_out).start()
+        third_copy(first, block, 0, landing, group_out).start()
+
+    def third_total(first, block, level, summed, landing):
+        third_copy(first, block, level, summed, landing).wait()
+        kept_rows = third_source(level, summed, landing)[
+            block, third_rows(level, third_bit(level)), :
+        ]
+        here = pl.ds(third_start(level), BLOCK >> (level + 1))
+        return kept_rows.astype(F32) + landing[block, here, :].astype(F32)
+
+    def stage_pass(first, block, summed, landing):
+        for level in range(levels - 1):
+            here = pl.ds(third_start(level), BLOCK >> (level + 1))
+            landing[block, here, :] = third_total(first, block, level, summed, landing).astype(BF16)
+            third_copy(first, block, level + 1, summed, landing).start()
 
     def stage_third(first, block, summed, landing):
-        mine = pl.ds(pl.multiple_of(third * share, share), share)
-        total = summed[block, mine, :].astype(F32)
-        for hop in range(1, thirds):
-            third_copy(first, block, hop, summed, landing).wait()
-            total = total + landing[block, hop - 1].astype(F32)
-        return total
+        return third_total(first, block, levels - 1, summed, landing)
 
     def gain_copy(stage, slot, device):
         return remote(
@@ -420,8 +457,7 @@
 
         def block_step(block, carry):
             lhs, rhs = turned.at[lax.div(block, 2)], hidden_units.at[block]
-            first = core_copy(0, block, ffn_c, units)
-            stage_send(lhs, rhs, units, first)
+            stage_send(lhs, rhs, 0, block, ffn_c, units)
 
             @pl.when(block < 2)
             def _():
@@ -460,15 +496,14 @@
                     down_copy(1).start()
 
             stage_core(
-                lhs, rhs, units, first, ffn_c.at[block], second_copy(0, block, ffn_c, ffn_y)
+                lhs, rhs, 0, block, ffn_c, units, second_copy(0, block, ffn_c, ffn_y)
             )
             return carry
 
         lax.fori_loop(0, 2, block_step, 0)
         columns = 2 * width
-        first = core_copy(3, 0, att_c, columns)
-        stage_send(low_turned, back_out, columns, first)
-        stage_core(low_turned, back_out, columns, first, att_c.at[0], second_copy(3, 0, att_c, att_y))
+        stage_send(low_turned, back_out, 3, 0, att_c, columns)
+        stage_core(low_turned, back_out, 3, 0, att_c, columns, second_copy(3, 0, att_c, att_y))
         lax.fori_loop(2, 3, block_step, 0)
 
         def down_own(part, carry):
@@ -541,6 +576,7 @@
         lax.fori_loop(0, rows // BLOCK, prepare, 0)
         gain_copy(0, 0, sibling).start()
         stage_second(0, 1, ffn_c, ffn_y, ffn_z)
+        stage_pass(0, 0, ffn_y, ffn_z)
 
         def by_query(block, carry):
             place, span = chunk(block), pl.ds(pl.multiple_of(block * BLOCK, BLOCK), SPAN)
@@ -601,6 +637,7 @@
         lax.fori_loop(0, rows // BLOCK, by_key, 0)
         lax.fori_loop(1, 2, finish_out, 0)
         stage_second(3, 0, att_c, att_y, att_z)
+        stage_pass(0, 1, ffn_y, ffn_z)
         for copy in later:
             copy.wait()
 
@@ -639,15 +676,15 @@
         def block_step(step, carry):
             block = step + 1
             rhs = pulls.at[step]
-            first = core_copy(3, block, att_c, columns)
-            stage_send(turned, rhs, columns, first)
+            stage_send(turned, rhs, 3, block, att_c, columns)
             stage_core(
-                turned, rhs, columns, first, att_c.at[block], second_copy(3, block, att_c, att_y)
+                turned, rhs, 3, block, att_c, columns, second_copy(3, block, att_c, att_y)
             )
 
             @pl.when(step == 0)
             def _():
                 stage_second(0, 2, ffn_c, ffn_y, ffn_z)
+                stage_pass(3, 0, att_y, att_z)
 
             return carry
 
@@ -669,6 +706,7 @@
 
             return carry
 
+        stage_pass(0, 2, ffn_y, ffn_z)
         lax.fori_loop(0, 1, attn_total, 0)
         turn_out[...] = attn_ref[0, :, width:].astype(BF16)
         turn_copy = over_x(25, turn_out, turn_in)
@@ -691,6 +729,11 @@
 
         def seconds_last(block, carry):
             stage_second(3, block, att_c, att_y, att_z)
+
+            @pl.when(block == 2)
+            def _():
+                stage_pass(3, 1, att_y, att_z)
+
             return carry
 
         lax.fori_loop(1, 3, seconds_last, 0)
@@ -701,6 +744,7 @@
             return carry
 
         lax.fori_loop(0, 3, ffn_total, 0)
+        stage_pass(3, 2, att_y, att_z)
         lax.fori_loop(1, 3, attn_total, 0)
         total = gain_sum[2]
         for hop in range(1, thirds):
@@ -764,9 +808,9 @@
         ((half, features), BF16), ((half, features), BF16),
         ((rows, width), BF16), (lane_rows, F32), ((half, features), BF16), ((share, width), BF16),
         ((3, 2 * quarter, units), BF16), ((3, quarter, units), BF16),
-        ((3, thirds - 1, share, units), BF16),
+        ((3, quarter - share, units), BF16),
         ((3, 2 * quarter, 2 * width), BF16), ((3, quarter, 2 * width), BF16),
-        ((3, thirds - 1, share, 2 * width), BF16), ((thirds + 1, 8, width), F32),
+        ((3, quarter - share, 2 * width), BF16), ((thirds + 1, 8, width), F32),
         ((1, rows + 2 * BAND), F32), (lane_rows, F32), ((rows, width), BF16),
         ((width, features), BF16), ((half, width), BF16),
         ((half, features), BF16), ((half, features), F32), ((half, features), F32),
@@ -785,7 +829,7 @@
         scratch_shapes=[pltpu.VMEM(size, dtype) for size, dtype in scratch]
         + [
             pltpu.SemaphoreType.DMA((27,)), pltpu.SemaphoreType.DMA((27,)),
-            pltpu.SemaphoreType.DMA((2, 6)), pltpu.SemaphoreType.DMA((2, 6)),
+            pltpu.SemaphoreType.DMA((3, 6)), pltpu.SemaphoreType.DMA((3, 6)),
             pltpu.SemaphoreType.DMA((7, thirds + 1)), pltpu.SemaphoreType.DMA((7, thirds + 1)),
             pltpu.SemaphoreType.DMA((12,)), pltpu.SemaphoreType.DMA((7,)),
         ],

time: 172 us -> 168 us (0.977)
  Pallas kernels: 170 us -> 167 us
    pallas_call x1, Pallas kernels: 164 us -> 161 us  [run_layer(): pl.pallas_call(functools.partial(layer, ways), in_specs=[vmem, pl.BlockSp...]
where the time goes in v6:
time: 168 us
  Pallas kernels  167 us (99%)
    pallas_call x1, Pallas kernels, run_layer(): pl.pallas_call(functools.partial(layer, ways), in_specs=[vmem, pl.BlockSp...  161 us
    pallas_call x1, Pallas kernels, run_finish(): pl.pallas_call(functools.partial(finish, ways), in_specs=[hbm] * 4 + [vme...  6.02 us

profile of v6, /device:TPU:0, one launch (start us, length us, event | category | flops | bytes accessed | tf_op | source)
XLA Modules:
  0.0 168.0 jit_solution(3132424780778787778)
XLA Ops:
  0.6 161.2 %layer.1 = (bf16[1024,1024]{1,0:T(8,128)(2,1)}, bf16[1024,1024]{1,0:T(8,128)(2,1)}, f32[3,64,1408]{2,1,0:T(8,128)}, f32[3,64,1024]{2,1,0:T(8,128)}, f32[8,512]{1...) custom-call(s32[1,1024]{1,0:T(1,128)} %ids_ref.1, ...), custom_call_target="tpu_custom_call" | custom-call | flops 49999998976 | bytes 62914560 | tf_op jit(solution)/shard_map/layer/pallas_call | solution.py:820
  161.9 6.0 %finish.1 = (bf16[1024,1024]{1,0:T(8,128)(2,1)}, f32[1024,1024]{1,0:T(8,128)}, f32[64,512]{1,0:T(8,128)}, f32[64,512]{1,0:T(8,128)}, f32[64,512]{1,0:T(8,128)}, ...) custom-call(bf16[1024,1024]{1,0:T(8,128)(2,1)} %get-tuple-element.27, ...), custom_call_target="tpu_custom_call" | custom-call | tf_op jit(solution)/shard_map/finish/pallas_call | solution.py:897

commit v7 on v6

--- a/solution.py
+++ b/solution.py
@@ -14,7 +14,7 @@
 SPAN = BAND + BLOCK
 F32 = jnp.float32
 BF16 = jnp.bfloat16
-VMEM_LIMIT = 62 * 1024 * 1024
+VMEM_LIMIT = 58 * 1024 * 1024
 
 
 def nn(left_op, right_op):
@@ -73,11 +73,11 @@
 def layer(
     ways,
     ids_ref, decay_ref, gain_ref, tok, cot, wo, wl, wr, wd, wq, wk, wv, wg,
-    out_ref, tg_ref, ffn_out, attn_out, gain_out,
+    out_ref, tg_ref, ffn_ref, attn_ref, gain_out,
     q, k, v, gate, heads, sq, sk,
-    u_in, wo_peer, sum_in, back_in, down_in, mixed_grad, cross, norm_in, turn_in,
+    u_in, wo_peer, sum_in, back_in, down_in, mixed_grad, cross, turn_in,
     ffn_c, ffn_y, ffn_z, att_c, att_y, att_z, gain_in,
-    seg_ref, sums_ref, u_all, wo_own, mixed_out, down_out, hidden, grad_hidden, scale_rows, core_out, gain_sum, turn_out,
+    seg_ref, sums_ref, u_all, wo_own, down_out, hidden, grad_hidden, scale_rows, core_out, gain_sum, turn_out,
     send, recv, dp_send, dp_recv, z_send, z_recv, local, kept,
 ):
     dp, side = lax.axis_index("dp"), lax.axis_index("tensor")
@@ -134,9 +134,8 @@
         return over_x(11 + part, source.at[chunk(part), :], back_in.at[chunk(part), :])
 
     def mixed_copy(part):
-        return over_x(
-            13 + part, mixed_out.at[chunk(part), :], mixed_grad.at[at(own0 + part * BLOCK), :]
-        )
+        place = at(own0 + part * BLOCK)
+        return over_x(13 + part, u_all.at[place, :], mixed_grad.at[place, :])
 
     def cross_copy(part):
         mine = cross.at[side * 2 + part]
@@ -146,13 +145,15 @@
         return over_x(17 + part, down_out.at[chunk(part), :], down_in.at[chunk(part), :])
 
     def norm_copy(source, part):
-        return over_x(19 + part, source.at[chunk(part), :], norm_in.at[chunk(part), :])
-
-    def out_copy(source, part):
-        return over_x(21 + part, source.at[chunk(part), :], out_ref.at[at(own0 + part * BLOCK), :])
-
-    def tg_copy(source, part):
-        return over_x(23 + part, source.at[chunk(part), :], tg_ref.at[at(own0 + part * BLOCK), :])
+        return over_x(19 + part, source.at[chunk(part), :], back_in.at[chunk(part), :])
+
+    def out_copy(part):
+        place = out_ref.at[at(own0 + part * BLOCK), :]
+        return over_x(21 + part, place, place)
+
+    def tg_copy(part):
+        place = tg_ref.at[at(own0 + part * BLOCK), :]
+        return over_x(23 + part, place, place)
 
     odd = lax.rem(third, 2)
     paired = ((third + 1 - 2 * odd) * 4 + second * 2 + core, side)
@@ -472,9 +473,7 @@
                 low = grad.astype(BF16)
                 for_own = nt(low, wo_own[...])
                 for_peer = nt(low, wo_peer[...])
-                mixed_out[chunk(part), :] = for_peer.astype(BF16)
                 mixed_grad[at(own0 + part * BLOCK), :] = for_own.astype(BF16)
-                mixed_copy(part).start()
                 place = at(own0 + part * BLOCK)
                 both = jnp.sum(
                     u_all[place, :].astype(F32) * for_own + u_in[place, :].astype(F32) * for_peer,
@@ -484,11 +483,13 @@
                 lanes = to_rows(both)
                 for i in range(lanes_in):
                     cross[side * 2 + part, i : i + 1, :] = lanes[i : i + 1, :]
-                cross_copy(part).start()
-                put_turned(low_turned, low, chunk(part))
                 scale = lane_column(scale_rows, side * 2 + part)
                 back_out[chunk(part), :width] = (u_all[place, :].astype(F32) * scale).astype(BF16)
                 back_out[chunk(part), width:] = (u_in[place, :].astype(F32) * scale).astype(BF16)
+                u_all[place, :] = for_peer.astype(BF16)
+                mixed_copy(part).start()
+                cross_copy(part).start()
+                put_turned(low_turned, low, chunk(part))
 
                 @pl.when(part == 1)
                 def _():
@@ -528,7 +529,7 @@
         pltpu.VMEM((features, half), BF16),
     )
 
-    def last(q_all, grads, k_all, v_all, slope_q, slope_k, heads_all, gate_all, pulls, weights, norm_out, norm_own, results, turned, tok_all, ffn_ref, attn_ref):
+    def last(q_all, grads, k_all, v_all, slope_q, slope_k, heads_all, gate_all, pulls, weights, norm_out, norm_own, turned, tok_all):
         columns = 2 * width
         loads = [
             load(0, v, v_all.at[pl.ds(BAND, rows), :]),
@@ -598,13 +599,10 @@
 
         def finish_out(part, carry):
             down_copy(part).wait()
-            results[0, chunk(part), :] = (
+            out_ref[at(own0 + part * BLOCK), :] = (
                 hidden[chunk(part), :] + down_in[chunk(part), :].astype(F32)
             ).astype(BF16)
-            out_copy(results.at[0], part).start()
-            pltpu.make_async_copy(
-                results.at[0, chunk(part), :], out_ref.at[at(own0 + part * BLOCK), :], local.at[part]
-            ).start()
+            out_copy(part).start()
             return carry
 
         lax.fori_loop(0, rows // BLOCK, by_query, 0)
@@ -694,16 +692,8 @@
         for hop in range(1, thirds):
             gain_copy(2, 1 + hop, far(hop)).start()
 
-        def attn_copy(block):
-            return pltpu.make_async_copy(attn_ref.at[block], attn_out.at[block], local.at[7 + block])
-
         def attn_total(block, carry):
             attn_ref[block] = stage_third(3, block, att_y, att_z)
-
-            @pl.when(block > 0)
-            def _():
-                attn_copy(block).start()
-
             return carry
 
         stage_pass(0, 2, ffn_y, ffn_z)
@@ -714,15 +704,12 @@
 
         def finish_tokens(part, carry):
             norm_copy(norm_out, part).wait()
-            pulled = norm_own[chunk(part), :] + norm_in[chunk(part), :].astype(F32)
+            pulled = norm_own[chunk(part), :] + back_in[chunk(part), :].astype(F32)
             source = tok_all[at(own0 + part * BLOCK), :].astype(F32)
-            results[1, chunk(part), :] = (
+            tg_ref[at(own0 + part * BLOCK), :] = (
                 grad_hidden[chunk(part), :] + rms_back(source, rms_scale(source), pulled)
             ).astype(BF16)
-            tg_copy(results.at[1], part).start()
-            pltpu.make_async_copy(
-                results.at[1, chunk(part), :], tg_ref.at[at(own0 + part * BLOCK), :], local.at[2 + part]
-            ).start()
+            tg_copy(part).start()
             return carry
 
         lax.fori_loop(0, 2, finish_tokens, 0)
@@ -740,7 +727,6 @@
 
         def ffn_total(block, carry):
             ffn_ref[block] = stage_third(0, block, ffn_y, ffn_z)
-            pltpu.make_async_copy(ffn_ref.at[block], ffn_out.at[block], local.at[4 + block]).start()
             return carry
 
         lax.fori_loop(0, 3, ffn_total, 0)
@@ -753,23 +739,10 @@
         gain_out[...] = total
         turn_copy.wait()
         attn_ref[0, :, :width] += turn_in[...].astype(F32)
-        attn_copy(0).start()
-
-        def close(part, carry):
-            out_copy(results.at[0], part).wait()
-            tg_copy(results.at[1], part).wait()
-            for index, target in ((0, out_ref), (1, tg_ref)):
-                pltpu.make_async_copy(
-                    results.at[index, chunk(part), :],
-                    target.at[at(own0 + part * BLOCK), :],
-                    local.at[2 * index + part],
-                ).wait()
-            return carry
-
-        lax.fori_loop(0, 2, close, 0)
-        for block in range(3):
-            pltpu.make_async_copy(ffn_ref.at[block], ffn_out.at[block], local.at[4 + block]).wait()
-            attn_copy(block).wait()
+
+        for part in range(2):
+            out_copy(part).wait()
+            tg_copy(part).wait()
 
     pl.run_scoped(
         last,
@@ -785,11 +758,8 @@
         pltpu.VMEM((features, 4 * width), BF16),
         pltpu.VMEM((half, features), BF16),
         pltpu.VMEM((half, features), F32),
-        pltpu.VMEM((2, half, features), BF16),
         pltpu.VMEM((features, rows), BF16),
         pltpu.VMEM((rows, features), BF16),
-        pltpu.VMEM(ffn_out.shape, F32),
-        pltpu.VMEM(attn_out.shape, F32),
     )
 
 
@@ -806,13 +776,13 @@
     scratch = [
         ((rows, width), BF16), ((width, features), BF16), (lane_rows, F32),
         ((half, features), BF16), ((half, features), BF16),
-        ((rows, width), BF16), (lane_rows, F32), ((half, features), BF16), ((share, width), BF16),
+        ((rows, width), BF16), (lane_rows, F32), ((share, width), BF16),
         ((3, 2 * quarter, units), BF16), ((3, quarter, units), BF16),
         ((3, quarter - share, units), BF16),
         ((3, 2 * quarter, 2 * width), BF16), ((3, quarter, 2 * width), BF16),
         ((3, quarter - share, 2 * width), BF16), ((thirds + 1, 8, width), F32),
         ((1, rows + 2 * BAND), F32), (lane_rows, F32), ((rows, width), BF16),
-        ((width, features), BF16), ((half, width), BF16),
+        ((width, features), BF16),
         ((half, features), BF16), ((half, features), F32), ((half, features), F32),
         (lane_rows, F32), ((2 * quarter, max(units, 2 * width)), BF16), ((3, 8, width), F32),
         ((share, width), BF16),
@@ -820,10 +790,11 @@
     return pl.pallas_call(
         functools.partial(layer, ways),
         in_specs=[vmem, pl.BlockSpec(memory_space=pltpu.SMEM), vmem] + [hbm] * (len(args) - 3),
-        out_specs=[hbm] * 4 + [vmem] + [hbm] * 7,
+        out_specs=[vmem] * 5 + [hbm] * 7,
         out_shape=[
-            shape((rows, features), BF16), shape((rows, features), BF16),
-            shape((3, share, units), F32), shape((3, share, 2 * width), F32), shape((8, width), F32),
+            pltpu.VMEM((rows, features), BF16), pltpu.VMEM((rows, features), BF16),
+            pltpu.VMEM((3, share, units), F32), pltpu.VMEM((3, share, 2 * width), F32),
+            pltpu.VMEM((8, width), F32),
         ]
         + [shape((rows, width), BF16)] * 7,
         scratch_shapes=[pltpu.VMEM(size, dtype) for size, dtype in scratch]
@@ -844,29 +815,25 @@
 def finish(
     ways, out_in, tg_in, ffn, attn, gain_in,
     out, tg, query, key, value, gate, output, gain, left, right, down,
-    out_held, tg_low, tg_wide, ffn_held, attn_held, arrived, left_here,
+    tg_wide, stored,
 ):
     width = query.shape[1]
     blocks = 2
     size = tg.shape[0] // blocks
     places = [pl.ds(i * size, size) for i in range(blocks)]
-    pairs = [(tg_in.at[i, :], tg_low.at[i, :], tg_wide.at[i, :], tg.at[i, :]) for i in places]
-    pairs += [(out_in.at[i, :], out_held.at[i, :], out_held.at[i, :], out.at[i, :]) for i in places]
-    for i, target in enumerate((left, right, down)):
-        pairs.append((ffn.at[i], ffn_held.at[i], ffn_held.at[i], target))
-    for i, j, target in ((1, 0, query), (1, 1, key), (2, 0, value), (2, 1, gate), (0, 0, output)):
-        cut = pl.ds(j * width, width)
-        held = attn_held.at[i, :, cut]
-        pairs.append((attn.at[i, :, cut], held, held, target))
-    loads = [
-        pltpu.make_async_copy(source, held, arrived.at[i])
-        for i, (source, held, _, _) in enumerate(pairs)
+    pairs = [(tg_wide.at[i, :], tg.at[i, :]) for i in places]
+    pairs.append((out_in, out))
+    pairs += [(ffn.at[i], target) for i, target in enumerate((left, right, down))]
+    cuts = [(1, 0, query), (1, 1, key), (2, 0, value), (2, 1, gate), (0, 0, output)]
+    pairs += [(attn.at[i, :, pl.ds(j * width, width)], target) for i, j, target in cuts]
+    stores = [
+        pltpu.make_async_copy(held, target, stored.at[i]) for i, (held, target) in enumerate(pairs)
     ]
-    stores = [
-        pltpu.make_async_copy(held, target, left_here.at[i])
-        for i, (_, _, held, target) in enumerate(pairs)
-    ]
-    for copy in loads:
+    stores[blocks].start()
+    for i in range(blocks):
+        tg_wide[places[i], :] = tg_in[places[i], :].astype(F32)
+        stores[i].start()
+    for copy in stores[blocks + 1 :]:
         copy.start()
     heads, each = gain.shape
     rows_in = jnp.concatenate([gain_in[0:1, i * 128 : i * 128 + 128] for i in range(heads)], axis=0)
@@ -878,11 +845,6 @@
         column = jnp.sum(jnp.where(lane == first + i, rows_in, 0.0), axis=1, keepdims=True)
         found = jnp.where(place == i, column, found)
     gain[...] = found
-    for i in range(len(pairs)):
-        loads[i].wait()
-        if i < blocks:
-            tg_wide[places[i], :] = tg_low[places[i], :].astype(F32)
-        stores[i].start()
     for copy in stores:
         copy.wait()
 
@@ -893,22 +855,18 @@
     vmem = pl.BlockSpec(memory_space=pltpu.VMEM)
     hbm = pl.BlockSpec(memory_space=pl.ANY)
     shape = lambda *size: jax.ShapeDtypeStruct(size, F32)
-    copies = 12
     return pl.pallas_call(
         functools.partial(finish, ways),
-        in_specs=[hbm] * 4 + [vmem],
+        in_specs=[vmem] * 5,
         out_specs=[hbm] * 7 + [vmem] + [hbm] * 3,
         out_shape=[jax.ShapeDtypeStruct((rows, features), BF16), shape(rows, features)]
         + [shape(share, width)] * 5
         + [shape(heads, gain_in.shape[1] // heads // ways)]
         + [shape(share, units)] * 3,
         scratch_shapes=[
-            pltpu.VMEM((rows, features), BF16), pltpu.VMEM((rows, features), BF16),
-            pltpu.VMEM((rows, features), F32), pltpu.VMEM((3, share, units), F32),
-            pltpu.VMEM((3, share, 2 * width), F32),
-            pltpu.SemaphoreType.DMA((copies,)), pltpu.SemaphoreType.DMA((copies,)),
+            pltpu.VMEM((rows, features), F32), pltpu.SemaphoreType.DMA((11,)),
         ],
-        compiler_params=pltpu.CompilerParams(vmem_limit_bytes=VMEM_LIMIT),
+        compiler_params=pltpu.CompilerParams(vmem_limit_bytes=16 * 1024 * 1024),
         name="finish",
     )(out_in, tg_in, ffn, attn, gain_in)
 

time: 168 us -> 165 us (0.982)
  Pallas kernels: 167 us -> 164 us
    pallas_call x1, Pallas kernels: 6.02 us -> 3.84 us  [run_finish(): pl.pallas_call(functools.partial(finish, ways), in_specs=[vmem] * 5, out_...]
where the time goes in v7:
time: 165 us
  Pallas kernels  164 us (99%)
    pallas_call x1, Pallas kernels, run_layer(): pl.pallas_call(functools.partial(layer, ways), in_specs=[vmem, pl.BlockSp...  161 us
    pallas_call x1, Pallas kernels, run_finish(): pl.pallas_call(functools.partial(finish, ways), in_specs=[vmem] * 5, out_...  3.84 us

profile of v7, /device:TPU:0, one launch (start us, length us, event | category | flops | bytes accessed | tf_op | source)
XLA Modules:
  0.0 165.2 jit_solution(12902881680285378670)
XLA Ops:
  0.6 160.6 %layer.1 = (bf16[1024,1024]{1,0:T(8,128)(2,1)S(1)}, bf16[1024,1024]{1,0:T(8,128)(2,1)S(1)}, f32[3,64,1408]{2,1,0:T(8,128)S(1)}, f32[3,64,1024]{2,1,0:T(8,128)S(1...) custom-call(s32[1,1024]{1,0:T(1,128)} %ids_ref.1, ...), custom_call_target="tpu_custom_call" | custom-call | flops 49999998976 | bytes 62914560 | tf_op jit(solution)/shard_map/layer/pallas_call | solution.py:790
  161.3 3.8 %finish.1 = (bf16[1024,1024]{1,0:T(8,128)(2,1)}, f32[1024,1024]{1,0:T(8,128)}, f32[64,512]{1,0:T(8,128)}, f32[64,512]{1,0:T(8,128)}, f32[64,512]{1,0:T(8,128)}, ...) custom-call(bf16[1024,1024]{1,0:T(8,128)(2,1)S(1)} %get-tuple-elemen, ...), custom_call_target="tpu_custom_call" | custom-call | tf_op jit(solution)/shard_map/finish/pallas_call | solution.py:858
